TPU v7x, 512 devices: a whole 4x8x8 slice. The times are simulated.
512 devices in a mesh: freq: 4 (over x), span: 16 (over z, core), wall: 8 (over y).
Axes of the slice: x: 4, y: 8, z: 8, core: 2. Of those that a mesh axis runs over, the one named last changes fastest.
Arguments:
- amplitudes: float32 [2, 5, 512, 32768], P(None, None, 'wall', ('freq', 'span')), may hold values from -20 to 20
- upstream: float32 [2, 5, 512, 32768], P(None, None, 'wall', ('freq', 'span')), may hold values from -6 to 6
- harmonic_mask: int32 [32768], P(('freq', 'span')), may hold values 0 or 1
- quadratic_coefficients: float32 [5, 5, 5], replicated, may hold values from -1.25 to 1.25
- slab_inverse: float32 [8, 320, 320], P('wall'), may hold values from -1 to 2
- lower_coupling: float32 [8, 5, 5], P('wall'), may hold values from -2.5 to 2.5
- upper_coupling: float32 [8, 5, 5], P('wall'), may hold values from -2.5 to 2.5
- reduced_lower: float32 [8, 10, 10], P('wall'), may hold values from -1 to 1
- reduced_upper: float32 [8, 10, 10], P('wall'), may hold values from -1 to 1
- reduced_pivot: float32 [8, 10, 10], P('wall'), may hold values from -2 to 3
Outputs:
- new_amplitudes: float32 [2, 5, 512, 32768], P(None, None, 'wall', ('freq', 'span'))
- wavenumber_shift: float32 [2, 32768], P(None, ('freq', 'span'))
Inputs may be any that keep to these rules, and one draw needn't show every extreme that they name: `harmonic_mask`: 1 marks a retained mode.
All inputs are finite; a program needn't handle non-finite values. No bound on the sum of `harmonic_mask` on one device may be relied on, other than what follows from the above.
Results may differ from a plain program's by a relative error of at most 0.0001.
Values sent between devices are 32-bit elements; how exact they have to be, the bound alone decides.
A program may use at most 64 MiB of HBM per device.

v0:
```python
import math

import jax
import jax.numpy as jnp
from jax import lax
from jax.sharding import PartitionSpec as P

NF = 128
NB = 256


epsilon = 1e-06


def carried_in(x, axis, combine, identity, reverse):
    count, place = (lax.axis_size(axis), lax.axis_index(axis))
    everything = jax.tree.map(lambda part: lax.all_gather(part, axis), x)
    start = jax.tree.map(
        lambda part, zero: jnp.broadcast_to(jnp.asarray(zero, part.dtype), part.shape), x, identity
    )

    def hop(k, before):
        at = count - 1 - k if reverse else k
        reached = at > place if reverse else at < place
        new = combine(before, jax.tree.map(lambda part: part[at], everything))
        return jax.tree.map(lambda a, b: jnp.where(reached, a, b), new, before)

    return lax.fori_loop(0, count, hop, start)


def shifted(block, axis, distance):
    devices = range(lax.axis_size(axis))
    route = [(i - distance, i) for i in devices if i - distance in devices]
    return lax.ppermute(block, axis, route)


def apply_left(matrix, vectors):
    return jnp.einsum("ij,cjm->cim", matrix, vectors, precision=lax.Precision.HIGHEST)


def compose(earlier, later):
    early_matrix, early_offset = earlier
    late_matrix, late_offset = later
    return (
        jnp.dot(late_matrix, early_matrix, precision=lax.Precision.HIGHEST),
        late_offset + apply_left(late_matrix, early_offset),
    )


def phase_table(rows, cols, length):
    phases = rows[:, None] * cols[None, :] % length
    angles = phases.astype(jnp.float32) * (2.0 * math.pi / length)
    return (jnp.cos(angles), jnp.sin(angles))


def quadratic(field, coefficients):
    weights = coefficients * (1.0 - jnp.eye(coefficients.shape[0], dtype=jnp.float32))[None]
    total = jnp.zeros_like(field)
    for source_var in range(field.shape[0]):
        mixed = jnp.einsum(
            "wb,bynt->wynt", weights[:, source_var, :], field, precision=lax.Precision.HIGHEST
        )
        total = total + field[source_var][None] * mixed
    return total


def time_field(pencil, table):
    return jnp.einsum("cvykz,ckt->vytz", pencil, table, precision=lax.Precision.HIGHEST)


def time_spectrum(forced, table):
    return jnp.einsum("vytz,dtk->dvykz", forced, table, precision=lax.Precision.HIGHEST)


def span_apply(values, table):
    return jnp.einsum("cvykl,cdlz->dvykz", values, table, precision=lax.Precision.HIGHEST)


def local(
    amplitudes,
    upstream,
    harmonic_mask,
    quadratic_coefficients,
    slab_inverse,
    lower_coupling,
    upper_coupling,
    reduced_lower,
    reduced_upper,
    reduced_pivot,
):
    variables = amplitudes.shape[1]
    heights = amplitudes.shape[2]
    pairs = amplitudes.shape[3]
    freq_local = pairs // NB
    keep = harmonic_mask.astype(jnp.float32)
    kept = amplitudes * keep
    weight_local = jnp.sum(kept * kept, axis=(0, 1, 2))
    weight_total = lax.psum(weight_local, "wall")
    scale = 1.0 / math.sqrt(NF * NB)
    counter = jnp.arange(NF, dtype=jnp.int32)
    cos_time, sin_time = phase_table(counter, counter, NF)
    time_forward = jnp.stack([cos_time, -sin_time])
    span_counter = jnp.arange(NB, dtype=jnp.int32)
    cos_span, sin_span = phase_table(span_counter, span_counter, NB)
    span_inverse = jnp.stack([jnp.stack([cos_span, sin_span]), jnp.stack([-sin_span, cos_span])])
    span_forward = (
        jnp.stack([jnp.stack([cos_span, -sin_span]), jnp.stack([sin_span, cos_span])]) * scale
    )
    spectral = span_apply(kept.reshape(2, variables, heights, freq_local, NB), span_inverse)
    freq_count = lax.axis_size("freq")
    span_count = lax.axis_size("span")
    outer = counter // (freq_count * freq_local)
    inner = counter // freq_local % freq_count
    received = (inner * span_count + outer) * freq_local + counter % freq_local
    cos_in, sin_in = phase_table(received, counter, NF)
    time_inverse = jnp.stack([cos_in, -sin_in]) * scale
    pencil = lax.all_to_all(
        lax.all_to_all(spectral, "freq", split_axis=2, concat_axis=3, tiled=True),
        "span",
        split_axis=2,
        concat_axis=3,
        tiled=True,
    )
    forced = quadratic(time_field(pencil, time_inverse), quadratic_coefficients)
    gathered_back = lax.all_to_all(
        lax.all_to_all(
            time_spectrum(forced, time_forward), "freq", split_axis=3, concat_axis=2, tiled=True
        ),
        "span",
        split_axis=3,
        concat_axis=2,
        tiled=True,
    )
    piece_rows = heights // (freq_count * span_count)
    reordered = gathered_back.reshape(
        2, variables, span_count, freq_count, piece_rows, freq_local, NB
    )
    returned = jnp.swapaxes(reordered, 2, 3).reshape(2, variables, heights, freq_local, NB)
    forcing = span_apply(returned, span_forward).reshape(2, variables, heights, pairs)
    right_side = (forcing + upstream) * keep
    inverse = slab_inverse[0]
    solved = apply_left(inverse, right_side.reshape(2, variables * heights, pairs))
    grid = solved.reshape(2, variables, heights, pairs)
    bounds = jnp.concatenate([grid[:, :, 0], grid[:, :, heights - 1]], axis=1)
    identity = (jnp.eye(2 * variables, dtype=jnp.float32), jnp.zeros_like(bounds))
    lower_block = reduced_lower[0]
    upper_block = reduced_upper[0]
    pivot_block = reduced_pivot[0]
    _, before = carried_in((-lower_block, bounds), "wall", compose, identity, False)
    ahead = bounds - apply_left(lower_block, before)
    step_matrix = -jnp.dot(pivot_block, upper_block, precision=lax.Precision.HIGHEST)
    _, after = carried_in(
        (step_matrix, apply_left(pivot_block, ahead)), "wall", compose, identity, True
    )
    interface = apply_left(pivot_block, ahead - apply_left(upper_block, after))
    below = shifted(interface[:, variables:], "wall", 1)
    above = after[:, :variables]
    columns = inverse.reshape(variables * heights, variables, heights)
    pushed = apply_left(columns[:, :, 0], apply_left(lower_coupling[0], below))
    pushed = pushed + apply_left(columns[:, :, heights - 1], apply_left(upper_coupling[0], above))
    new_amplitudes = (solved - pushed).reshape(2, variables, heights, pairs)
    change = new_amplitudes - kept
    real_part = jnp.sum(kept[0] * change[0] + kept[1] * change[1], axis=(0, 1))
    imag_part = jnp.sum(kept[0] * change[1] - kept[1] * change[0], axis=(0, 1))
    real_total, imag_total = lax.psum((real_part, imag_part), "wall")
    weight = weight_total + epsilon
    wavenumber_shift = jnp.stack([imag_total / weight, -real_total / weight])
    return (new_amplitudes, wavenumber_shift)


def solution(mesh):
    placed = (
        P(None, None, "wall", ("freq", "span")),
        P(None, None, "wall", ("freq", "span")),
        P(("freq", "span")),
        P(),
        P("wall", None, None),
        P("wall", None, None),
        P("wall", None, None),
        P("wall", None, None),
        P("wall", None, None),
        P("wall", None, None),
    )
    return jax.shard_map(
        local,
        mesh=mesh,
        in_specs=placed,
        out_specs=(P(None, None, "wall", ("freq", "span")), P(None, ("freq", "span"))),
        check_vma=False,
    )
```

profile of v0, /device:TPU:64, one launch (start us, length us, event | category | flops | bytes accessed | tf_op | source)
XLA Modules:
  0.0 261.6 jit_solution(10588118522992166869)
XLA Ops:
  0.6 1.7 fusion.89
  2.4 1.7 fusion.91
  4.0 0.7 convert_element_type.77
  4.7 1.6 multiply_reduce_fusion
  6.3 0.8 reshape.379
  7.1 2.1 fusion.73
  9.3 2.3 convolution_bitcast_fusion.4
  11.5 1.0 copy.84
  12.5 22.0 %all_to_all.54 = f32[2,5,64,2,256]{4,3,1,0,2:T(2,128)S(1)} all-to-all(f32[2,5,64,2,256]{4,3,1,0,2:T(2,128)S(1)} %copy.84), channel_id=1, replica_groups=mesh['freq'=4,'span'=16,'wall'=8] {'freq'}, dimensions={2} | all-to-all | bytes 2621440 | tf_op jit(solution)/shard_map/all_to_all | solution.py:118
  34.9 1.8 copy.87
  36.8 10.1 %all-to-all-start.1 = ((f32[2,5,16,8,256]{4,3,1,0,2:T(8,128)}), f32[2,5,16,8,256]{4,3,1,0,2:T(8,128)S(1)}, u32[]{:S(2)}, u32[]{:S(2)}) async-start(f32[2,5,16,8,256]{4,3,1,0,2:T(8,128)} %copy.87), calls=%async_computation.1 | async-start | bytes 2621440 | tf_op jit(solution)/shard_map/all_to_all | solution.py:117
  46.9 0.3 sine_negate_fusion.1
  47.2 0.3 fusion.107
  47.5 29.6 %all-to-all-done.1 = f32[2,5,16,8,256]{4,3,1,0,2:T(8,128)S(1)} async-done(((f32[2,5,16,8,256]{4,3,1,0,2:T(8,128)}), f32[2,5,16,8,256]{4,3,1,0,2:T(8,128)S(1)}, u32[]{:S(2)}, u32[]{:S(2)}) %all-to-all-start.1) | async-done | bytes 1310752 | tf_op jit(solution)/shard_map/all_to_all | solution.py:117
  77.1 0.8 fusion.57
  78.0 1.3 fusion.45
  79.3 1.3 fusion.48
  80.7 1.3 fusion.51
  82.0 1.3 fusion.54
  83.4 1.6 fusion.42
  85.0 1.3 convolution_bitcast_fusion.3
  86.3 1.0 copy.96
  87.3 21.2 %all_to_all.55 = f32[2,5,1,128,256]{4,0,2,1,3:T(2,128)S(1)} all-to-all(f32[2,5,1,128,256]{4,0,2,1,3:T(2,128)S(1)} %copy.96), channel_id=1, replica_groups=mesh['freq'=4,'span'=16,'wall'=8] {'freq'}, dimensions={3} | all-to-all | bytes 2621440 | tf_op jit(solution)/shard_map/all_to_all | solution.py:126
  108.6 1.9 copy.97
  110.5 6.7 %all-to-all-start.3 = ((f32[2,5,4,32,256]{4,2,1,0,3:T(4,128)}), f32[2,5,4,32,256]{4,2,1,0,3:T(4,128)S(1)}, u32[]{:S(2)}, u32[]{:S(2)}) async-start(f32[2,5,4,32,256]{4,2,1,0,3:T(4,128)} %copy.97), calls=%async_computation.3 | async-start | bytes 2621440 | tf_op jit(solution)/shard_map/all_to_all | solution.py:125
  117.1 2.0 copy.104
  119.2 26.2 %all_gather.24 = f32[8,10,10]{2,1,0:T(8,128)S(1)} all-gather(f32[1,10,10]{2,1,0:T(8,128)S(1)} %copy_negate_fusion), channel_id=1, replica_groups=mesh['freq'=4,'span'=16,'wall'=8] {'wall'}, dimensions={0}, use_global_device_ids=true | all-gather | bytes 3600 | tf_op jit(solution)/shard_map/all_gather | solution.py:17
  145.5 24.6 %all-gather.3 = f32[8,10,10]{2,1,0:T(8,128)S(1)} all-gather(f32[1,10,10]{2,1,0:T(8,128)S(1)} %fusion.64), channel_id=4, replica_groups=mesh['freq'=4,'span'=16,'wall'=8] {'wall'}, dimensions={0}, use_global_device_ids=true | all-gather | bytes 3600 | tf_op jit(solution)/shard_map/all_gather | solution.py:17
  170.1 0.9 fusion.125
  171.0 0.8 copy.98
  172.0 2.3 convolution_bitcast_fusion.2
  174.5 1.1 copy-done.3
  175.6 0.3 add_multiply_fusion
  175.9 0.7 copy-done.2
  176.6 2.3 fusion.75
  179.0 25.5 %all-gather = f32[16,10,512]{2,1,0:T(8,128)S(1)} all-gather(f32[2,10,512]{2,1,0:T(8,128)S(1)} %pad_maximum_fusion.4), channel_id=2, replica_groups=mesh['freq'=4,'span'=16,'wall'=8] {'wall'}, dimensions={0}, use_global_device_ids=true | all-gather | bytes 368640 | tf_op jit(solution)/shard_map/all_gather | solution.py:17
  204.6 1.9 while.30
  206.9 25.3 %all-gather.1 = f32[16,10,512]{2,1,0:T(8,128)S(1)} all-gather(f32[2,10,512]{2,1,0:T(8,128)S(1)} %convolution_bitcast_fusion.7), channel_id=3, replica_groups=mesh['freq'=4,'span'=16,'wall'=8] {'wall'}, dimensions={0}, use_global_device_ids=true | all-gather | bytes 368640 | tf_op jit(solution)/shard_map/all_gather | solution.py:17
  232.3 2.0 while.31
  234.7 2.6 %collective-permute-start = (f32[2,5,512]{2,1,0:T(8,128)S(1)}, f32[2,5,512]{2,1,0:T(8,128)S(1)}, u32[]{:S(2)}, u32[]{:S(2)}) collective-permute-start(f32[2,5,512]{2,1,0:T(8,128)S(1)} %slice.96), channel_id=1, source_target_pairs={{0,1},{1,2},{2,3},{3,4},{4,5},{5,6},{6,7},{8,9},{9,10},{10,11},{11... | collective-permute-start | bytes 61448 | tf_op jit(solution)/shard_map/ppermute | solution.py:34
  237.5 1.4 collective-permute-done
  239.1 1.2 fusion.109
  240.3 1.3 fusion.29
  241.7 0.3 sub.53
  242.0 0.8 copy-done
  242.7 0.3 subtract_reduce_fusion
  243.1 17.9 %all-reduce = (f32[512]{0:T(512)S(1)}, f32[512]{0:T(512)S(1)}, f32[512]{0:T(512)S(1)}) all-reduce(f32[512]{0:T(512)S(1)} %get-tuple-element.267, f32[512]{0:T(512)S(1)} %get-tuple-element.291, f32[512]{0:T(512)S(1)} %get-tuple-element.266), channel_id=1, replica_groups=mesh['freq'=4,'span'=16,'wall'=8] {'wall'}, use_global_device_ids=true, to_apply=%region_9.10 | all-reduce | flops 1536 | bytes 12288 | tf_op jit(solution)/shard_map/psum | solution.py:165
  261.0 0.6 pad_maximum_fusion.5
  (73 shorter events, 5.6 us)
Async XLA Ops:
  36.8 10.4 %copy-start.7 = (f32[5,5,5]{2,1,0:T(8,128)S(1)}, f32[5,5,5]{2,1,0:T(8,128)}, u32[]{:S(2)}) copy-start(f32[5,5,5]{2,1,0:T(8,128)} %param.17) | copy-start | bytes 1504
  36.8 40.3 %all-to-all-start.1 = ((f32[2,5,16,8,256]{4,3,1,0,2:T(8,128)}), f32[2,5,16,8,256]{4,3,1,0,2:T(8,128)S(1)}, u32[]{:S(2)}, u32[]{:S(2)}) async-start(f32[2,5,16,8,256]{4,3,1,0,2:T(8,128)} %copy.87), calls=%async_computation.1 | async-start | bytes 2621440 | tf_op jit(solution)/shard_map/all_to_all | solution.py:117
  110.5 8.7 %copy-start.6 = (f32[1,10,10]{2,0,1:T(1,128)S(1)}, f32[1,10,10]{2,0,1:T(1,128)}, u32[]{:S(2)}) copy-start(f32[1,10,10]{2,0,1:T(1,128)} %param.21) | copy-start | bytes 1204
  110.5 34.9 %copy-start.4 = (f32[1,10,10]{2,0,1:T(1,128)S(1)}, f32[1,10,10]{2,0,1:T(1,128)}, u32[]{:S(2)}) copy-start(f32[1,10,10]{2,0,1:T(1,128)} %param.23) | copy-start | bytes 1204
  110.5 34.9 %copy-start.5 = (f32[1,10,10]{2,0,1:T(1,128)S(1)}, f32[1,10,10]{2,0,1:T(1,128)}, u32[]{:S(2)}) copy-start(f32[1,10,10]{2,0,1:T(1,128)} %param.22) | copy-start | bytes 1204
  110.5 60.5 %all-to-all-start.3 = ((f32[2,5,4,32,256]{4,2,1,0,3:T(4,128)}), f32[2,5,4,32,256]{4,2,1,0,3:T(4,128)S(1)}, u32[]{:S(2)}, u32[]{:S(2)}) async-start(f32[2,5,4,32,256]{4,2,1,0,3:T(4,128)} %copy.97), calls=%async_computation.3 | async-start | bytes 2621440 | tf_op jit(solution)/shard_map/all_to_all | solution.py:125
  170.9 1.0 copy-start.1
  174.3 1.3 copy-start.3
  175.6 1.0 copy-start.2
  232.3 5.1 %copy-start.8 = (f32[1,5,5]{2,0,1:T(1,128)S(1)}, f32[1,5,5]{2,0,1:T(1,128)}, u32[]{:S(2)}) copy-start(f32[1,5,5]{2,0,1:T(1,128)} %param.20) | copy-start | bytes 304
  232.3 6.6 %copy-start.9 = (f32[1,5,5]{2,0,1:T(1,128)S(1)}, f32[1,5,5]{2,0,1:T(1,128)}, u32[]{:S(2)}) copy-start(f32[1,5,5]{2,0,1:T(1,128)} %param.19) | copy-start | bytes 304
  234.7 4.2 %collective-permute-start = (f32[2,5,512]{2,1,0:T(8,128)S(1)}, f32[2,5,512]{2,1,0:T(8,128)S(1)}, u32[]{:S(2)}, u32[]{:S(2)}) collective-permute-start(f32[2,5,512]{2,1,0:T(8,128)S(1)} %slice.96), channel_id=1, source_target_pairs={{0,1},{1,2},{2,3},{3,4},{4,5},{5,6},{6,7},{8,9},{9,10},{10,11},{11... | collective-permute-start | bytes 61448 | tf_op jit(solution)/shard_map/ppermute | solution.py:34
  241.7 1.1 copy-start
where the time goes:
time: 262 us
  blocking collectives  163 us (62%)
  waiting for transfers between devices  31 us (12%)
  matrix products  23 us (9%)
  starting transfers between devices  19.4 us (7%)
  local copies, waits for them, and re-layouts  13.9 us (5%)
  other arithmetic  9.88 us (4%)
    all_gather x4, blocking collectives, carried_in(): everything = jax.tree.map(lambda part: lax.all_gather(part, axis), x)  102 us
    all_to_all x1, waiting for transfers between devices, local(): lax.all_to_all(lax.all_to_all(spectral, 'freq', split_axis=2, concat_axis...  29.6 us
    all_to_all x1, blocking collectives, local(): lax.all_to_all(spectral, 'freq', split_axis=2, concat_axis=3, tiled=True)  22 us
    all_to_all x1, blocking collectives, local(): lax.all_to_all(time_spectrum(forced, time_forward), 'freq', split_axis=3,...  21.2 us
    psum x1, blocking collectives, local(): real_total, imag_total = lax.psum((real_part, imag_part), 'wall')  17.9 us
    all_to_all x1, starting transfers between devices, local(): lax.all_to_all(lax.all_to_all(spectral, 'freq', split_axis=2, concat_axis...  10.1 us
    dot_general x25, matrix products, apply_left(): jnp.einsum('ij,cjm->cim', matrix, vectors, precision=lax.Precision.HIGHEST)  9.21 us
    dot_general x5, matrix products, quadratic(): jnp.einsum('wb,bynt->wynt', weights[:, source_var, :], field, precision=l...  6.99 us
  transfers between devices with their start and end apart: 3, of which 2 were waited for; matrix products, arithmetic and copies ran while one was open for 1% of the time, Pallas kernels for 0%

commit v1 on v0

v1 whole, which is shorter than its diff:
```python
import functools
import math

import jax
import jax.numpy as jnp
import numpy as np
from jax import lax
from jax.experimental import pallas as pl
from jax.experimental.pallas import tpu as pltpu
from jax.sharding import PartitionSpec as P

MESH = pl.DeviceIdType.MESH
V = 5
CY = 64
NF = 128
NB = 256
GROUP = 64
WALL = 8
LANES = 2 * V * CY
MESSAGE = 8 * V
EXT = V * CY
epsilon = 1e-06
HIGHEST = lax.Precision.HIGHEST
NT = (((1,), (1,)), ((), ()))
NN = (((1,), (0,)), ((), ()))


def split(x):
    high = x.astype(jnp.bfloat16)
    low = (x - high.astype(jnp.float32)).astype(jnp.bfloat16)
    return high, low


def product(a, b, dims):
    (ah, al), (bh, bl) = a, b
    dot = functools.partial(
        lax.dot_general, dimension_numbers=dims, preferred_element_type=jnp.float32
    )
    return dot(ah, bh) + (dot(ah, bl) + dot(al, bh))


def exact(a, b, dims=NN):
    return lax.dot_general(
        a, b, dimension_numbers=dims, precision=HIGHEST, preferred_element_type=jnp.float32
    )


def tables():
    scale = 1.0 / math.sqrt(NF * NB)
    n = np.arange(2 * NB)
    z = 4 * (n // 8) + n % 4
    d = (n // 4) % 2
    phase = 2.0 * np.pi * ((z[:, None] * np.arange(NB)[None, :]) % NB) / NB
    cos, sin = np.cos(phase), np.sin(phase)
    odd = (d == 1)[:, None]
    span = np.concatenate([np.where(odd, sin, cos), np.where(odd, cos, -sin)], axis=1)
    j, t = np.arange(GROUP), np.arange(GROUP)
    inverse, forward = [], []
    for r in range(2):
        phase = 2.0 * np.pi * ((t[:, None] * (2 * j + r)[None, :]) % NF) / NF
        pair = np.concatenate([np.cos(phase), -np.sin(phase)], axis=1) * scale
        inverse.append(pair)
        forward.append(pair.T)
    out = []
    for table in (span, np.concatenate(inverse, axis=1), np.concatenate(forward, axis=1)):
        table = table.astype(np.float32)
        high = table.astype(jnp.bfloat16)
        low = (table - high.astype(np.float32)).astype(jnp.bfloat16)
        out += [high, low]
    return out


def kernel(
    amp_ref, up_ref, mask_ref, quad_ref, inv_ref, lower_ref, upper_ref, rlow_ref, rup_ref, rpiv_ref,
    th_ref, tl_ref, ch_ref, cl_ref, dh_ref, dl_ref,
    new_ref, shift_ref,
    kh, kl, send1, recv1, send2, recv2, invs, ph, pl_, su, et, acc, zmat, nmat, mm,
    wsend, wrecv, msend, mrecv, bsend, brecv, lsend, lrecv, nsend, nrecv, invb_h, invb_l,
    s1, r1, s2, r2, sw, rw,
):
    f, s, w = lax.axis_index("freq"), lax.axis_index("span"), lax.axis_index("wall")
    chip, core = s // 2, s % 2
    me = f * 16 + s
    barrier = pltpu.get_barrier_semaphore()

    def peer(i):
        i = jnp.where(i >= 7, i + 1, i)
        n = 7 - i % 8
        dz = (n % 2) * ((n + 1) // 2) + (1 - n % 2) * ((8 - n // 2) % 8)
        df, dc = (i // 8) % 4, i // 32
        return (f + df) % 4, ((chip + dz) % 8) * 2 + (core + dc) % 2

    def greet(i, carry):
        pf, ps = peer(i)
        pl.semaphore_signal(barrier, inc=1, device_id={"freq": pf, "span": ps}, device_id_type=MESH)
        return carry

    lax.fori_loop(0, GROUP - 1, greet, 0)
    for i in range(1, WALL):
        pl.semaphore_signal(barrier, inc=1, device_id={"wall": (w + i) % WALL}, device_id_type=MESH)

    def tile(index):
        return pl.ds(pl.multiple_of(MESSAGE * index, 8), MESSAGE)

    def exchange(src, dst, ssem, rsem):
        def go(i, carry):
            pf, ps = peer(i)
            p = pf * 16 + ps
            pltpu.make_async_remote_copy(
                src_ref=src.at[tile(p)], dst_ref=dst.at[tile(me)], send_sem=ssem.at[p],
                recv_sem=rsem.at[me], device_id={"freq": pf, "span": ps}, device_id_type=MESH,
            ).start()
            return carry

        lax.fori_loop(0, GROUP - 1, go, 0)

    def finish(src, dst, ssem, rsem):
        def done(i, carry):
            pf, ps = peer(i)
            p = pf * 16 + ps
            pltpu.make_async_remote_copy(
                src_ref=src.at[tile(p)], dst_ref=dst.at[tile(p)], send_sem=ssem.at[p],
                recv_sem=rsem.at[p], device_id={"freq": pf, "span": ps}, device_id_type=MESH,
            ).wait()
            return carry

        lax.fori_loop(0, GROUP - 1, done, 0)

    def wall_copy(step, i, src, dst, inbound=False):
        p = (w + i) % WALL
        return pltpu.make_async_remote_copy(
            src_ref=src(p), dst_ref=dst.at[p if inbound else w], send_sem=sw.at[step, p],
            recv_sem=rw.at[step, p if inbound else w], device_id={"wall": p}, device_id_type=MESH,
        )

    keep = mask_ref[...].astype(jnp.float32)

    weight = jnp.zeros((1, 2 * NB), jnp.float32)
    for c in range(2):
        for v in range(V):
            block = amp_ref[c, v] * keep
            weight = weight + jnp.sum(block * block, axis=0, keepdims=True)
            high, low = split(block)
            for r in range(2):
                rows = pl.ds(v * 2 * CY + r * CY, CY)
                cols = pl.ds(c * NB, NB)
                kh[rows, cols] = high[:, r * NB : (r + 1) * NB]
                kl[rows, cols] = low[:, r * NB : (r + 1) * NB]

    def spectral(q, carry):
        rows = pl.ds(pl.multiple_of(128 * q, 128), 128)
        found = product((th_ref[rows, :], tl_ref[rows, :]), (kh[...], kl[...]), NT)
        for p in range(16):
            for v in range(V):
                at = pl.multiple_of(16 * MESSAGE * q + MESSAGE * p + 8 * v, 8)
                send1[pl.ds(at, 8), :] = found[8 * p : 8 * p + 8, 128 * v : 128 * v + 128]
        return carry

    lax.fori_loop(0, 4, spectral, 0)
    pl.semaphore_wait(barrier, GROUP - 1 + WALL - 1)
    exchange(send1, recv1, s1, r1)
    recv1[tile(me), :] = send1[tile(me), :]

    msend[...] = jnp.zeros_like(msend)
    msend[0:10, 0:10] = rlow_ref[0]
    msend[16:26, 0:10] = rup_ref[0]
    msend[32:42, 0:10] = rpiv_ref[0]
    for q in range(4):
        msend[48 + q : 49 + q, :] = weight[:, 128 * q : 128 * (q + 1)]
    for i in range(1, WALL):
        wall_copy(0, i, lambda p: msend, mrecv).start()
    mrecv[w] = msend[...]

    invs[...] = jnp.zeros_like(invs)
    invs[:, 0:EXT] = inv_ref[0]
    row = lax.broadcasted_iota(jnp.int32, (16, 384), 0)
    col = lax.broadcasted_iota(jnp.int32, (16, 384), 1)
    ends = jnp.zeros((16, 384), jnp.float32)
    for v in range(V):
        for q in range(V):
            first = (row == q) & (col == v * CY)
            last = (row == V + q) & (col == v * CY + CY - 1)
            ends = jnp.where(first, lower_ref[0, v, q], ends)
            ends = jnp.where(last, upper_ref[0, v, q], ends)
    et[...] = ends
    zt = exact(et[...], invs[...], NT)
    zmat[...] = exact(invs[...], et[...], NT)
    for c in range(2):
        kept = (amp_ref[c] * keep).reshape(EXT, 2 * NB)
        found = exact(zt, kept)
        for q in range(4):
            wsend[q, c] = found[:, 128 * q : 128 * (q + 1)]
    for i in range(1, WALL):
        wall_copy(1, i, lambda p: wsend.at[p % 4], wrecv).start()
    wrecv[w] = wsend[w % 4]

    lower_half = lax.broadcasted_iota(jnp.int32, (EXT, 128), 1) < CY
    for v in range(V):
        here = invs[:, 128 * (v // 2) : 128 * (v // 2) + 128]
        there = pltpu.roll(here, CY, 1)
        for r in range(2):
            inside = lower_half if r == 0 else jnp.logical_not(lower_half)
            high, low = split(jnp.where(inside, here if v % 2 == r else there, 0.0))
            ph[r, :, 128 * v : 128 * (v + 1)] = high
            pl_[r, :, 128 * v : 128 * (v + 1)] = low
    inv_h, inv_l = split(inv_ref[0])
    for c in range(2):
        source = split(up_ref[c].reshape(EXT, 2 * NB))
        su[:, c * 2 * NB : (c + 1) * 2 * NB] = product((inv_h, inv_l), source, NN)

    for i in range(1, WALL):
        wall_copy(0, i, lambda p: msend, mrecv, True).wait()
    row = lax.broadcasted_iota(jnp.int32, (16, 128), 0)
    col = lax.broadcasted_iota(jnp.int32, (16, 128), 1)
    ahead = []
    for i in range(WALL):
        unit = jnp.where((col == 16 * i + row) & (row < 2 * V), 1.0, 0.0)
        ahead.append(unit if i == 0 else unit - exact(mrecv[i, 0:16, 0:16], ahead[-1]))
    interface = [None] * WALL
    for i in range(WALL - 1, -1, -1):
        value = ahead[i]
        if i < WALL - 1:
            value = value - exact(mrecv[i, 16:32, 0:16], interface[i + 1])
        interface[i] = exact(mrecv[i, 32:48, 0:16], value)
    for i in range(WALL):
        need = jnp.zeros((16, 128), jnp.float32)
        if i > 0:
            need = jnp.where(row < V, pltpu.roll(interface[i - 1], 16 - V, 0), need)
        if i < WALL - 1:
            need = jnp.where((row >= V) & (row < 2 * V), pltpu.roll(interface[i + 1], V, 0), need)
        mm[16 * i : 16 * (i + 1), :] = need
    total_weight = mrecv[0, 48:56, :]
    for i in range(1, WALL):
        total_weight = total_weight + mrecv[i, 48:56, :]
    for i in range(1, WALL):
        wall_copy(1, i, lambda p: wsend.at[p % 4], wrecv, True).wait()

    finish(send1, recv1, s1, r1)
    half = lax.broadcasted_iota(jnp.int32, (GROUP, 128), 1) < CY
    sign = jnp.where(half, 1.0, -1.0)
    wide = lax.broadcasted_iota(jnp.int32, (128, LANES), 1) % 128 < CY
    halves = lax.broadcasted_iota(jnp.int32, (GROUP, LANES), 1) % 128 < CY
    for z in range(4):
        picked = jnp.concatenate([
            jnp.concatenate([
                recv1[pl.ds(8 * v + 4 * d + z, GROUP, stride=MESSAGE), :] for v in range(V)
            ], axis=1) for d in range(2)
        ], axis=0)
        stacked = jnp.concatenate(
            [jnp.where(wide, picked, 0.0), jnp.where(wide, 0.0, picked)], axis=0
        )
        mixed = product((ch_ref[...], cl_ref[...]), split(stacked), NN)
        field = []
        for v in range(V):
            x = mixed[:, 128 * v : 128 * (v + 1)]
            field.append(pltpu.roll(x, CY, 1) + sign * x)
        force = [jnp.zeros((GROUP, 128), jnp.float32) for _ in range(V)]
        for a in range(V):
            for b in range(a + 1, V):
                both = field[a] * field[b]
                for o in range(V):
                    force[o] = force[o] + (quad_ref[o, a, b] + quad_ref[o, b, a]) * both
        folded = jnp.concatenate([pltpu.roll(x, CY, 1) + sign * x for x in force], axis=1)
        stacked = jnp.concatenate(
            [jnp.where(halves, folded, 0.0), jnp.where(halves, 0.0, folded)], axis=0
        )
        back = product((dh_ref[...], dl_ref[...]), split(stacked), NN)
        for v in range(V):
            for d in range(2):
                send2[pl.ds(8 * v + 4 * d + z, GROUP, stride=MESSAGE), :] = back[
                    GROUP * d : GROUP * (d + 1), 128 * v : 128 * (v + 1)
                ]
    exchange(send2, recv2, s2, r2)
    recv2[tile(me), :] = send2[tile(me), :]

    for r in range(2):
        invb_h[r] = jnp.zeros((16, LANES), jnp.bfloat16)
        invb_l[r] = jnp.zeros((16, LANES), jnp.bfloat16)
        for v in range(V):
            for e in range(2):
                at = v * CY + e * (CY - 1)
                invb_h[r, e * V + v : e * V + v + 1, :] = ph[r, at : at + 1, :]
                invb_l[r, e * V + v : e * V + v + 1, :] = pl_[r, at : at + 1, :]
    finish(send2, recv2, s2, r2)

    landed = recv2[...].reshape(GROUP, V, 8, 128)
    arrived = split(
        jnp.concatenate([landed[:, v].reshape(2 * NB, 128) for v in range(V)], axis=1)
    )
    table = (th_ref[...], tl_ref[...])
    for r in range(2):
        edge = product((invb_h[r], invb_l[r]), arrived, NT)
        edge = product(split(edge), table, NN)
        for c in range(2):
            for q in range(2):
                at = r * NB + q * 128
                part = edge[:, c * NB + q * 128 : c * NB + (q + 1) * 128]
                for e in range(2):
                    for v in range(V):
                        o = v * CY + e * (CY - 1)
                        bsend[c * 4 + r * 2 + q, e * V + v : e * V + v + 1, :] = (
                            part[e * V + v : e * V + v + 1, :]
                            + su[o : o + 1, c * 2 * NB + at : c * 2 * NB + at + 128]
                        ) * keep[:, at : at + 128]
    for q in range(WALL):
        bsend[q, 2 * V : 16, :] = jnp.zeros((16 - 2 * V, 128), jnp.float32)
    for i in range(1, WALL):
        wall_copy(2, i, lambda p: bsend.at[p], brecv).start()
    brecv[w] = bsend[w]

    for r in range(2):
        solved = product(split(product((ph[r], pl_[r]), arrived, NT)), table, NN)
        for c in range(2):
            at = c * 2 * NB + r * NB
            acc[:, at : at + NB] = (
                solved[:, c * NB : (c + 1) * NB] + su[:, at : at + NB]
            ) * keep[:, r * NB : (r + 1) * NB]
    real = jnp.zeros((1, 2 * NB), jnp.float32)
    imag = jnp.zeros((1, 2 * NB), jnp.float32)
    for v in range(V):
        rows = slice(v * CY, (v + 1) * CY)
        k0, k1 = amp_ref[0, v] * keep, amp_ref[1, v] * keep
        c0, c1 = acc[rows, 0 : 2 * NB] - k0, acc[rows, 2 * NB : 4 * NB] - k1
        real = real + jnp.sum(k0 * c0 + k1 * c1, axis=0, keepdims=True)
        imag = imag + jnp.sum(k0 * c1 - k1 * c0, axis=0, keepdims=True)
    for q in range(4):
        lsend[q : q + 1, :] = real[:, 128 * q : 128 * (q + 1)]
        lsend[4 + q : 5 + q, :] = imag[:, 128 * q : 128 * (q + 1)]
    for i in range(1, WALL):
        wall_copy(3, i, lambda p: lsend, lrecv).start()
    lrecv[w] = lsend[...]

    for i in range(1, WALL):
        wall_copy(2, i, lambda p: bsend.at[p], brecv, True).wait()
    need = exact(mm[...], brecv[...].reshape(16 * WALL, 128))
    part = w // 4
    same = wrecv[:, part].reshape(16 * WALL, 128)
    other = wrecv[:, 1 - part].reshape(16 * WALL, 128)
    turn = (2 * part - 1).astype(jnp.float32)
    real = jnp.sum(same * need, axis=0, keepdims=True)
    imag = jnp.sum(other * need, axis=0, keepdims=True) * turn
    nsend[...] = need.reshape(WALL, 16, 128)
    for i in range(WALL):
        nsend[i, 10:11, :] = real
        nsend[i, 11:12, :] = imag
    for i in range(1, WALL):
        wall_copy(4, i, lambda p: nsend.at[p], nrecv).start()
    nrecv[w] = nsend[w]
    for i in range(1, WALL):
        wall_copy(3, i, lambda p: lsend, lrecv, True).wait()
    inner = lrecv[0]
    for i in range(1, WALL):
        inner = inner + lrecv[i]
    for i in range(1, WALL):
        wall_copy(4, i, lambda p: nsend.at[p], nrecv, True).wait()

    for q in range(WALL):
        nmat[:, 128 * q : 128 * (q + 1)] = nrecv[q]
    zsplit = split(zmat[...])
    for c in range(2):
        cols = slice(c * 2 * NB, (c + 1) * 2 * NB)
        pushed = product(zsplit, split(nmat[:, cols]), NN)
        new_ref[c] = (acc[:, cols] - pushed).reshape(V, CY, 2 * NB)
    for q in range(4):
        real = inner[q : q + 1, :] - nrecv[q, 10:11, :] - nrecv[4 + q, 10:11, :]
        imag = inner[4 + q : 5 + q, :] - nrecv[q, 11:12, :] - nrecv[4 + q, 11:12, :]
        size = total_weight[q : q + 1, :] + epsilon
        shift_ref[0:1, 128 * q : 128 * (q + 1)] = imag / size
        shift_ref[1:2, 128 * q : 128 * (q + 1)] = -real / size


def solution(mesh):
    consts = tables()

    def local(
        amplitudes, upstream, harmonic_mask, quadratic_coefficients, slab_inverse,
        lower_coupling, upper_coupling, reduced_lower, reduced_upper, reduced_pivot,
    ):
        vmem = pl.BlockSpec(memory_space=pltpu.VMEM)
        smem = pl.BlockSpec(memory_space=pltpu.SMEM)
        f32, bf16 = jnp.float32, jnp.bfloat16
        modes = amplitudes.shape[3]
        return pl.pallas_call(
            kernel,
            out_shape=(
                jax.ShapeDtypeStruct(amplitudes.shape, f32),
                jax.ShapeDtypeStruct((2, modes), f32),
            ),
            in_specs=[vmem, vmem, vmem, smem, vmem, smem, smem, vmem, vmem, vmem] + [vmem] * 6,
            out_specs=(vmem, vmem),
            scratch_shapes=[
                pltpu.VMEM((LANES, 2 * NB), bf16),
                pltpu.VMEM((LANES, 2 * NB), bf16),
                pltpu.VMEM((GROUP * MESSAGE, 128), f32),
                pltpu.VMEM((GROUP * MESSAGE, 128), f32),
                pltpu.VMEM((GROUP * MESSAGE, 128), f32),
                pltpu.VMEM((GROUP * MESSAGE, 128), f32),
                pltpu.VMEM((EXT, 384), f32),
                pltpu.VMEM((2, EXT, LANES), bf16),
                pltpu.VMEM((2, EXT, LANES), bf16),
                pltpu.VMEM((EXT, 4 * NB), f32),
                pltpu.VMEM((16, 384), f32),
                pltpu.VMEM((EXT, 4 * NB), f32),
                pltpu.VMEM((EXT, 16), f32),
                pltpu.VMEM((16, 4 * NB), f32),
                pltpu.VMEM((128, 128), f32),
                pltpu.VMEM((4, 2, 16, 128), f32),
                pltpu.VMEM((WALL, 2, 16, 128), f32),
                pltpu.VMEM((56, 128), f32),
                pltpu.VMEM((WALL, 56, 128), f32),
                pltpu.VMEM((WALL, 16, 128), f32),
                pltpu.VMEM((WALL, 16, 128), f32),
                pltpu.VMEM((8, 128), f32),
                pltpu.VMEM((WALL, 8, 128), f32),
                pltpu.VMEM((WALL, 16, 128), f32),
                pltpu.VMEM((WALL, 16, 128), f32),
                pltpu.VMEM((2, 16, LANES), bf16),
                pltpu.VMEM((2, 16, LANES), bf16),
                pltpu.SemaphoreType.DMA((GROUP,)),
                pltpu.SemaphoreType.DMA((GROUP,)),
                pltpu.SemaphoreType.DMA((GROUP,)),
                pltpu.SemaphoreType.DMA((GROUP,)),
                pltpu.SemaphoreType.DMA((5, WALL)),
                pltpu.SemaphoreType.DMA((5, WALL)),
            ],
            compiler_params=pltpu.CompilerParams(
                collective_id=0, has_side_effects=True, vmem_limit_bytes=60 << 20
            ),
        )(
            amplitudes, upstream, harmonic_mask.reshape(1, modes), quadratic_coefficients,
            slab_inverse, lower_coupling, upper_coupling, reduced_lower, reduced_upper,
            reduced_pivot, *[jnp.asarray(table) for table in consts],
        )

    placed = (
        P(None, None, "wall", ("freq", "span")),
        P(None, None, "wall", ("freq", "span")),
        P(("freq", "span")),
        P(),
        P("wall", None, None),
        P("wall", None, None),
        P("wall", None, None),
        P("wall", None, None),
        P("wall", None, None),
        P("wall", None, None),
    )
    return jax.shard_map(
        local,
        mesh=mesh,
        in_specs=placed,
        out_specs=(P(None, None, "wall", ("freq", "span")), P(None, ("freq", "span"))),
        check_vma=False,
    )
```

time: 262 us -> 115 us (0.44)
  the two profiles are of different devices: /device:TPU:64 before, /device:TPU:1 now
where the time goes in v1:
time: 115 us
  Pallas kernels  105 us (91%)
  local copies, waits for them, and re-layouts  9.46 us (8%)
    pallas_call x1, Pallas kernels, local(): pl.pallas_call(kernel, out_shape=(jax.ShapeDtypeStruct(amplitudes.shape,...  105 us
    unnamed x9, local copies, waits for them, and re-layouts  9.46 us

profile of v1, /device:TPU:1, one launch (start us, length us, event | category | flops | bytes accessed | tf_op | source)
XLA Modules:
  0.0 114.8 jit_solution(4935053427931226495)
XLA Ops:
  0.6 1.3 %copy.18.lower_ref = f32[1,5,5]{2,1,0:T(8,128)} copy(f32[1,5,5]{2,0,1:T(1,128)} %param.21) | data formatting | bytes 200 | tf_op args[5]
  1.9 1.3 %copy.19.upper_ref = f32[1,5,5]{2,1,0:T(8,128)} copy(f32[1,5,5]{2,0,1:T(1,128)} %param.22) | data formatting | bytes 200 | tf_op args[6]
  3.2 1.3 %copy.20.rlow_ref = f32[1,10,10]{2,1,0:T(8,128)} copy(f32[1,10,10]{2,0,1:T(1,128)} %param.23) | data formatting | bytes 800 | tf_op args[7]
  4.5 1.3 %copy.21.rup_ref = f32[1,10,10]{2,1,0:T(8,128)} copy(f32[1,10,10]{2,0,1:T(1,128)} %param.24) | data formatting | bytes 800 | tf_op args[8]
  5.7 1.3 %copy.22.rpiv_ref = f32[1,10,10]{2,1,0:T(8,128)} copy(f32[1,10,10]{2,0,1:T(1,128)} %param.25) | data formatting | bytes 800 | tf_op args[9]
  7.0 104.7 %shard_map.167 = (f32[2,5,64,512]{3,2,1,0:T(8,128)}, f32[2,512]{1,0:T(2,128)}) custom-call(f32[2,5,64,512]{3,2,1,0:T(8,128)} %amp_ref.1, f32[2,5,64,512]{3,2,1,0:T(8,128)} %up_ref.1, s32[1,512]{1,0:T(1,128)} %bitcast.1, f32[5,5,5]{2,1,0:T(8,128)} %quad_ref.1, f32[1,320,320]{2,1,0:T(8,128)} %inv_ref.1, f32[1,5,5]{2,1,0:T(8,128)} %copy.18.lower_ref, ...), custom_call_target="tpu_custom_call" | custom-call | tf_op jit(solution)/shard_map/pallas_call | solution.py:383
  111.7 0.0 copy-start
  111.7 2.5 %copy.25 = f32[2,5,64,512]{3,2,1,0:T(8,128)} copy(f32[2,5,64,512]{3,2,1,0:T(8,128)} %get-tuple-element.4) | data formatting | bytes 2621440
  114.2 0.0 copy-done
  114.2 0.6 copy.26
Async XLA Ops:
  111.7 2.5 %copy-start = (f32[2,512]{1,0:T(2,128)S(1)}, f32[2,512]{1,0:T(2,128)}, u32[]{:S(2)}) copy-start(f32[2,512]{1,0:T(2,128)} %get-tuple-element.5) | copy-start | bytes 12292

commit v2 on v1

--- a/solution.py
+++ b/solution.py
@@ -54,15 +54,17 @@
     cos, sin = np.cos(phase), np.sin(phase)
     odd = (d == 1)[:, None]
     span = np.concatenate([np.where(odd, sin, cos), np.where(odd, cos, -sin)], axis=1)
-    j, t = np.arange(GROUP), np.arange(GROUP)
+    t, place = np.arange(GROUP), np.arange(GROUP)
+    j = (place // 8 % 4) * 16 + (place % 8) * 2 + place // 32
     inverse, forward = [], []
     for r in range(2):
         phase = 2.0 * np.pi * ((t[:, None] * (2 * j + r)[None, :]) % NF) / NF
-        pair = np.concatenate([np.cos(phase), -np.sin(phase)], axis=1) * scale
-        inverse.append(pair)
-        forward.append(pair.T)
+        pair = np.stack([np.cos(phase), -np.sin(phase)], axis=1) * scale
+        inverse.append(pair.reshape(GROUP, 2, 2, 32))
+        forward.append(pair.reshape(GROUP, 2 * GROUP).T)
+    inverse = np.stack(inverse).transpose(3, 1, 0, 2, 4).reshape(2, GROUP, 2 * GROUP)
     out = []
-    for table in (span, np.concatenate(inverse, axis=1), np.concatenate(forward, axis=1)):
+    for table in (span, inverse, np.concatenate(forward, axis=1)):
         table = table.astype(np.float32)
         high = table.astype(jnp.bfloat16)
         low = (table - high.astype(np.float32)).astype(jnp.bfloat16)
@@ -71,28 +73,37 @@
 
 
 def kernel(
-    amp_ref, up_ref, mask_ref, quad_ref, inv_ref, lower_ref, upper_ref, rlow_ref, rup_ref, rpiv_ref,
-    th_ref, tl_ref, ch_ref, cl_ref, dh_ref, dl_ref,
-    new_ref, shift_ref,
-    kh, kl, send1, recv1, send2, recv2, invs, ph, pl_, su, et, acc, zmat, nmat, mm,
-    wsend, wrecv, msend, mrecv, bsend, brecv, lsend, lrecv, nsend, nrecv, invb_h, invb_l,
-    s1, r1, s2, r2, sw, rw,
+    amp_hbm, up_hbm, mask_ref, quad_ref, inv_hbm, lower_ref, upper_ref, rlow_ref, rup_ref, rpiv_ref,
+    th_hbm, tl_hbm, ch_ref, cl_ref, dh_ref, dl_ref,
+    acc_hbm, zmat, nrecv, inner_ref, weight_ref,
+    amp_ref, up_ref, inv_ref, th_ref, tl_ref,
+    kh, kl, send1, recv1, send2, recv2, invs, ph, pl_, su, et, acc, mixed, eacc, pacc, mm,
+    wsend, wrecv, msend, mrecv, bsend, brecv, lsend, lrecv, nsend, invb_h, invb_l,
+    s1, r1, s2, r2, sw, rw, loads,
 ):
     f, s, w = lax.axis_index("freq"), lax.axis_index("span"), lax.axis_index("wall")
     chip, core = s // 2, s % 2
-    me = f * 16 + s
+    me = core * 32 + f * 8 + chip
     barrier = pltpu.get_barrier_semaphore()
+
+    fetch = [
+        pltpu.make_async_copy(amp_hbm.at[:, v], amp_ref.at[:, v], loads.at[v]) for v in range(V)
+    ]
+    for src, dst in ((th_hbm, th_ref), (tl_hbm, tl_ref), (inv_hbm, inv_ref), (up_hbm, up_ref)):
+        fetch.append(pltpu.make_async_copy(src, dst, loads.at[len(fetch)]))
+    for copy in fetch:
+        copy.start()
 
     def peer(i):
         i = jnp.where(i >= 7, i + 1, i)
         n = 7 - i % 8
         dz = (n % 2) * ((n + 1) // 2) + (1 - n % 2) * ((8 - n // 2) % 8)
         df, dc = (i // 8) % 4, i // 32
-        return (f + df) % 4, ((chip + dz) % 8) * 2 + (core + dc) % 2
+        pf, pc, pz = (f + df) % 4, (core + dc) % 2, (chip + dz) % 8
+        return {"freq": pf, "span": pz * 2 + pc}, pc * 32 + pf * 8 + pz
 
     def greet(i, carry):
-        pf, ps = peer(i)
-        pl.semaphore_signal(barrier, inc=1, device_id={"freq": pf, "span": ps}, device_id_type=MESH)
+        pl.semaphore_signal(barrier, inc=1, device_id=peer(i)[0], device_id_type=MESH)
         return carry
 
     lax.fori_loop(0, GROUP - 1, greet, 0)
@@ -102,29 +113,36 @@
     def tile(index):
         return pl.ds(pl.multiple_of(MESSAGE * index, 8), MESSAGE)
 
-    def exchange(src, dst, ssem, rsem):
+    def message(i, src, dst, ssem, rsem, inbound):
+        device, p = peer(i)
+        at = p if inbound else me
+        return pltpu.make_async_remote_copy(
+            src_ref=src.at[tile(p)], dst_ref=dst.at[tile(at)], send_sem=ssem.at[p],
+            recv_sem=rsem.at[at], device_id=device, device_id_type=MESH,
+        )
+
+    def exchange(*args):
         def go(i, carry):
-            pf, ps = peer(i)
-            p = pf * 16 + ps
-            pltpu.make_async_remote_copy(
-                src_ref=src.at[tile(p)], dst_ref=dst.at[tile(me)], send_sem=ssem.at[p],
-                recv_sem=rsem.at[me], device_id={"freq": pf, "span": ps}, device_id_type=MESH,
-            ).start()
+            message(i, *args, False).start()
             return carry
 
         lax.fori_loop(0, GROUP - 1, go, 0)
 
-    def finish(src, dst, ssem, rsem):
+    def arrive(first, last, *args):
         def done(i, carry):
-            pf, ps = peer(i)
-            p = pf * 16 + ps
-            pltpu.make_async_remote_copy(
-                src_ref=src.at[tile(p)], dst_ref=dst.at[tile(p)], send_sem=ssem.at[p],
-                recv_sem=rsem.at[p], device_id={"freq": pf, "span": ps}, device_id_type=MESH,
-            ).wait()
+            message(i, *args, True).wait_recv()
             return carry
 
+        lax.fori_loop(first, last, done, 0)
+
+    def sent(*args):
+        def done(i, carry):
+            message(i, *args, True).wait_send()
+            return carry
+
         lax.fori_loop(0, GROUP - 1, done, 0)
+
+    parts = ((core, 0, 31), (1 - core, 31, GROUP - 1))
 
     def wall_copy(step, i, src, dst, inbound=False):
         p = (w + i) % WALL
@@ -136,8 +154,9 @@
     keep = mask_ref[...].astype(jnp.float32)
 
     weight = jnp.zeros((1, 2 * NB), jnp.float32)
-    for c in range(2):
-        for v in range(V):
+    for v in range(V):
+        fetch[v].wait()
+        for c in range(2):
             block = amp_ref[c, v] * keep
             weight = weight + jnp.sum(block * block, axis=0, keepdims=True)
             high, low = split(block)
@@ -147,6 +166,9 @@
                 kh[rows, cols] = high[:, r * NB : (r + 1) * NB]
                 kl[rows, cols] = low[:, r * NB : (r + 1) * NB]
 
+    fetch[V].wait()
+    fetch[V + 1].wait()
+
     def spectral(q, carry):
         rows = pl.ds(pl.multiple_of(128 * q, 128), 128)
         found = product((th_ref[rows, :], tl_ref[rows, :]), (kh[...], kl[...]), NT)
@@ -162,15 +184,16 @@
     recv1[tile(me), :] = send1[tile(me), :]
 
     msend[...] = jnp.zeros_like(msend)
-    msend[0:10, 0:10] = rlow_ref[0]
-    msend[16:26, 0:10] = rup_ref[0]
-    msend[32:42, 0:10] = rpiv_ref[0]
+    msend[0:10, 0:10] = rlow_ref[:, 0]
+    msend[16:26, 0:10] = rup_ref[:, 0]
+    msend[32:42, 0:10] = rpiv_ref[:, 0]
     for q in range(4):
         msend[48 + q : 49 + q, :] = weight[:, 128 * q : 128 * (q + 1)]
     for i in range(1, WALL):
         wall_copy(0, i, lambda p: msend, mrecv).start()
     mrecv[w] = msend[...]
 
+    fetch[V + 2].wait()
     invs[...] = jnp.zeros_like(invs)
     invs[:, 0:EXT] = inv_ref[0]
     row = lax.broadcasted_iota(jnp.int32, (16, 384), 0)
@@ -180,8 +203,8 @@
         for q in range(V):
             first = (row == q) & (col == v * CY)
             last = (row == V + q) & (col == v * CY + CY - 1)
-            ends = jnp.where(first, lower_ref[0, v, q], ends)
-            ends = jnp.where(last, upper_ref[0, v, q], ends)
+            ends = jnp.where(first, lower_ref[v, 0, q], ends)
+            ends = jnp.where(last, upper_ref[v, 0, q], ends)
     et[...] = ends
     zt = exact(et[...], invs[...], NT)
     zmat[...] = exact(invs[...], et[...], NT)
@@ -201,8 +224,9 @@
         for r in range(2):
             inside = lower_half if r == 0 else jnp.logical_not(lower_half)
             high, low = split(jnp.where(inside, here if v % 2 == r else there, 0.0))
-            ph[r, :, 128 * v : 128 * (v + 1)] = high
-            pl_[r, :, 128 * v : 128 * (v + 1)] = low
+            ph[r * EXT : (r + 1) * EXT, 128 * v : 128 * (v + 1)] = high
+            pl_[r * EXT : (r + 1) * EXT, 128 * v : 128 * (v + 1)] = low
+    fetch[V + 3].wait()
     inv_h, inv_l = split(inv_ref[0])
     for c in range(2):
         source = split(up_ref[c].reshape(EXT, 2 * NB))
@@ -232,27 +256,39 @@
     total_weight = mrecv[0, 48:56, :]
     for i in range(1, WALL):
         total_weight = total_weight + mrecv[i, 48:56, :]
+    weight_ref[...] = total_weight + epsilon
+    invb_h[...] = jnp.zeros_like(invb_h)
+    invb_l[...] = jnp.zeros_like(invb_l)
+    for r in range(2):
+        for e in range(2):
+            for v in range(V):
+                to, at = 16 * r + e * V + v, r * EXT + v * CY + e * (CY - 1)
+                invb_h[to : to + 1, :] = ph[at : at + 1, :]
+                invb_l[to : to + 1, :] = pl_[at : at + 1, :]
     for i in range(1, WALL):
         wall_copy(1, i, lambda p: wsend.at[p % 4], wrecv, True).wait()
 
-    finish(send1, recv1, s1, r1)
     half = lax.broadcasted_iota(jnp.int32, (GROUP, 128), 1) < CY
     sign = jnp.where(half, 1.0, -1.0)
-    wide = lax.broadcasted_iota(jnp.int32, (128, LANES), 1) % 128 < CY
     halves = lax.broadcasted_iota(jnp.int32, (GROUP, LANES), 1) % 128 < CY
+    for stage, (parity, first, last) in enumerate(parts):
+        arrive(first, last, send1, recv1, s1, r1)
+        for z in range(4):
+            picked = jnp.concatenate([
+                jnp.concatenate([
+                    recv1[pl.ds(32 * MESSAGE * parity + 8 * v + 4 * d + z, 32, stride=MESSAGE), :]
+                    for v in range(V)
+                ], axis=1) for d in range(2)
+            ], axis=0)
+            stacked = jnp.concatenate(
+                [jnp.where(halves, picked, 0.0), jnp.where(halves, 0.0, picked)], axis=0
+            )
+            found = product((ch_ref[parity], cl_ref[parity]), split(stacked), NN)
+            mixed[z] = found if stage == 0 else mixed[z] + found
     for z in range(4):
-        picked = jnp.concatenate([
-            jnp.concatenate([
-                recv1[pl.ds(8 * v + 4 * d + z, GROUP, stride=MESSAGE), :] for v in range(V)
-            ], axis=1) for d in range(2)
-        ], axis=0)
-        stacked = jnp.concatenate(
-            [jnp.where(wide, picked, 0.0), jnp.where(wide, 0.0, picked)], axis=0
-        )
-        mixed = product((ch_ref[...], cl_ref[...]), split(stacked), NN)
         field = []
         for v in range(V):
-            x = mixed[:, 128 * v : 128 * (v + 1)]
+            x = mixed[z, :, 128 * v : 128 * (v + 1)]
             field.append(pltpu.roll(x, CY, 1) + sign * x)
         force = [jnp.zeros((GROUP, 128), jnp.float32) for _ in range(V)]
         for a in range(V):
@@ -273,24 +309,25 @@
     exchange(send2, recv2, s2, r2)
     recv2[tile(me), :] = send2[tile(me), :]
 
+    sent(send1, recv1, s1, r1)
+    for stage, (parity, first, last) in enumerate(parts):
+        arrive(first, last, send2, recv2, s2, r2)
+        rows = pl.ds(pl.multiple_of(32 * MESSAGE * parity, 8), 32 * MESSAGE)
+        landed = recv2[rows, :].reshape(32, V, 8, 128)
+        arrived = split(
+            jnp.concatenate([landed[:, v].reshape(2 * 128, 128) for v in range(V)], axis=1)
+        )
+        rows = pl.ds(pl.multiple_of(256 * parity, 256), 256)
+        table = (th_ref[rows, :], tl_ref[rows, :])
+        found = product((invb_h[...], invb_l[...]), arrived, NT)
+        found = product(split(found), table, NN)
+        if stage == 0:
+            eacc[...] = found
+            found = product((ph[...], pl_[...]), arrived, NT)
+            pacc[...] = product(split(found), table, NN)
+    edges = eacc[...] + found
     for r in range(2):
-        invb_h[r] = jnp.zeros((16, LANES), jnp.bfloat16)
-        invb_l[r] = jnp.zeros((16, LANES), jnp.bfloat16)
-        for v in range(V):
-            for e in range(2):
-                at = v * CY + e * (CY - 1)
-                invb_h[r, e * V + v : e * V + v + 1, :] = ph[r, at : at + 1, :]
-                invb_l[r, e * V + v : e * V + v + 1, :] = pl_[r, at : at + 1, :]
-    finish(send2, recv2, s2, r2)
-
-    landed = recv2[...].reshape(GROUP, V, 8, 128)
-    arrived = split(
-        jnp.concatenate([landed[:, v].reshape(2 * NB, 128) for v in range(V)], axis=1)
-    )
-    table = (th_ref[...], tl_ref[...])
-    for r in range(2):
-        edge = product((invb_h[r], invb_l[r]), arrived, NT)
-        edge = product(split(edge), table, NN)
+        edge = edges[16 * r : 16 * (r + 1)]
         for c in range(2):
             for q in range(2):
                 at = r * NB + q * 128
@@ -308,13 +345,15 @@
         wall_copy(2, i, lambda p: bsend.at[p], brecv).start()
     brecv[w] = bsend[w]
 
+    pacc[...] += product(split(product((ph[...], pl_[...]), arrived, NT)), table, NN)
     for r in range(2):
-        solved = product(split(product((ph[r], pl_[r]), arrived, NT)), table, NN)
         for c in range(2):
             at = c * 2 * NB + r * NB
             acc[:, at : at + NB] = (
-                solved[:, c * NB : (c + 1) * NB] + su[:, at : at + NB]
+                pacc[r * EXT : (r + 1) * EXT, c * NB : (c + 1) * NB] + su[:, at : at + NB]
             ) * keep[:, r * NB : (r + 1) * NB]
+    store = pltpu.make_async_copy(acc, acc_hbm, loads.at[V + 4])
+    store.start()
     real = jnp.zeros((1, 2 * NB), jnp.float32)
     imag = jnp.zeros((1, 2 * NB), jnp.float32)
     for v in range(V):
@@ -351,22 +390,27 @@
     inner = lrecv[0]
     for i in range(1, WALL):
         inner = inner + lrecv[i]
+    inner_ref[...] = inner
+    sent(send2, recv2, s2, r2)
+    store.wait()
     for i in range(1, WALL):
         wall_copy(4, i, lambda p: nsend.at[p], nrecv, True).wait()
 
-    for q in range(WALL):
-        nmat[:, 128 * q : 128 * (q + 1)] = nrecv[q]
-    zsplit = split(zmat[...])
-    for c in range(2):
-        cols = slice(c * 2 * NB, (c + 1) * 2 * NB)
-        pushed = product(zsplit, split(nmat[:, cols]), NN)
-        new_ref[c] = (acc[:, cols] - pushed).reshape(V, CY, 2 * NB)
-    for q in range(4):
-        real = inner[q : q + 1, :] - nrecv[q, 10:11, :] - nrecv[4 + q, 10:11, :]
-        imag = inner[4 + q : 5 + q, :] - nrecv[q, 11:12, :] - nrecv[4 + q, 11:12, :]
-        size = total_weight[q : q + 1, :] + epsilon
-        shift_ref[0:1, 128 * q : 128 * (q + 1)] = imag / size
-        shift_ref[1:2, 128 * q : 128 * (q + 1)] = -real / size
+
+def update(acc_ref, zmat_ref, near_ref, inner_ref, weight_ref, new_ref, shift_ref):
+    near = split(jnp.concatenate([near_ref[q] for q in range(WALL)], axis=1))
+    value = acc_ref[...] - product(split(zmat_ref[...]), near, NN)
+    new_ref[0, 0] = value[:, 0 : 2 * NB]
+    new_ref[1, 0] = value[:, 2 * NB : 4 * NB]
+
+    @pl.when(pl.program_id(0) == 0)
+    def _():
+        for q in range(4):
+            real = inner_ref[q : q + 1, :] - near_ref[q, 10:11, :] - near_ref[4 + q, 10:11, :]
+            imag = inner_ref[4 + q : 5 + q, :] - near_ref[q, 11:12, :] - near_ref[4 + q, 11:12, :]
+            size = weight_ref[q : q + 1, :]
+            shift_ref[0:1, 128 * q : 128 * (q + 1)] = imag / size
+            shift_ref[1:2, 128 * q : 128 * (q + 1)] = -real / size
 
 
 def solution(mesh):
@@ -380,15 +424,29 @@
         smem = pl.BlockSpec(memory_space=pltpu.SMEM)
         f32, bf16 = jnp.float32, jnp.bfloat16
         modes = amplitudes.shape[3]
-        return pl.pallas_call(
+        hbm = pl.BlockSpec(memory_space=pl.ANY)
+
+        def turned(block):
+            return jnp.transpose(block, (1, 0, 2))
+
+        acc, zmat, near, inner, weight = pl.pallas_call(
             kernel,
             out_shape=(
-                jax.ShapeDtypeStruct(amplitudes.shape, f32),
-                jax.ShapeDtypeStruct((2, modes), f32),
+                jax.ShapeDtypeStruct((EXT, 4 * NB), f32),
+                jax.ShapeDtypeStruct((EXT, 16), f32),
+                jax.ShapeDtypeStruct((WALL, 16, 128), f32),
+                jax.ShapeDtypeStruct((8, 128), f32),
+                jax.ShapeDtypeStruct((8, 128), f32),
             ),
-            in_specs=[vmem, vmem, vmem, smem, vmem, smem, smem, vmem, vmem, vmem] + [vmem] * 6,
-            out_specs=(vmem, vmem),
+            in_specs=[hbm, hbm, vmem, smem, hbm, smem, smem, vmem, vmem, vmem]
+            + [hbm, hbm] + [vmem] * 4,
+            out_specs=(hbm, vmem, vmem, vmem, vmem),
             scratch_shapes=[
+                pltpu.VMEM((2, V, CY, 2 * NB), f32),
+                pltpu.VMEM((2, V, CY, 2 * NB), f32),
+                pltpu.VMEM((1, EXT, EXT), f32),
+                pltpu.VMEM((2 * NB, 2 * NB), bf16),
+                pltpu.VMEM((2 * NB, 2 * NB), bf16),
                 pltpu.VMEM((LANES, 2 * NB), bf16),
                 pltpu.VMEM((LANES, 2 * NB), bf16),
                 pltpu.VMEM((GROUP * MESSAGE, 128), f32),
@@ -396,13 +454,14 @@
                 pltpu.VMEM((GROUP * MESSAGE, 128), f32),
                 pltpu.VMEM((GROUP * MESSAGE, 128), f32),
                 pltpu.VMEM((EXT, 384), f32),
-                pltpu.VMEM((2, EXT, LANES), bf16),
-                pltpu.VMEM((2, EXT, LANES), bf16),
+                pltpu.VMEM((2 * EXT, LANES), bf16),
+                pltpu.VMEM((2 * EXT, LANES), bf16),
                 pltpu.VMEM((EXT, 4 * NB), f32),
                 pltpu.VMEM((16, 384), f32),
                 pltpu.VMEM((EXT, 4 * NB), f32),
-                pltpu.VMEM((EXT, 16), f32),
-                pltpu.VMEM((16, 4 * NB), f32),
+                pltpu.VMEM((4, GROUP, LANES), f32),
+                pltpu.VMEM((32, 2 * NB), f32),
+                pltpu.VMEM((2 * EXT, 2 * NB), f32),
                 pltpu.VMEM((128, 128), f32),
                 pltpu.VMEM((4, 2, 16, 128), f32),
                 pltpu.VMEM((WALL, 2, 16, 128), f32),
@@ -413,24 +472,45 @@
                 pltpu.VMEM((8, 128), f32),
                 pltpu.VMEM((WALL, 8, 128), f32),
                 pltpu.VMEM((WALL, 16, 128), f32),
-                pltpu.VMEM((WALL, 16, 128), f32),
-                pltpu.VMEM((2, 16, LANES), bf16),
-                pltpu.VMEM((2, 16, LANES), bf16),
+                pltpu.VMEM((32, LANES), bf16),
+                pltpu.VMEM((32, LANES), bf16),
                 pltpu.SemaphoreType.DMA((GROUP,)),
                 pltpu.SemaphoreType.DMA((GROUP,)),
                 pltpu.SemaphoreType.DMA((GROUP,)),
                 pltpu.SemaphoreType.DMA((GROUP,)),
                 pltpu.SemaphoreType.DMA((5, WALL)),
                 pltpu.SemaphoreType.DMA((5, WALL)),
+                pltpu.SemaphoreType.DMA((V + 5,)),
             ],
             compiler_params=pltpu.CompilerParams(
                 collective_id=0, has_side_effects=True, vmem_limit_bytes=60 << 20
             ),
         )(
             amplitudes, upstream, harmonic_mask.reshape(1, modes), quadratic_coefficients,
-            slab_inverse, lower_coupling, upper_coupling, reduced_lower, reduced_upper,
-            reduced_pivot, *[jnp.asarray(table) for table in consts],
+            slab_inverse, turned(lower_coupling), turned(upper_coupling), turned(reduced_lower),
+            turned(reduced_upper), turned(reduced_pivot),
+            *[jnp.asarray(table) for table in consts],
         )
+        whole = lambda shape: pl.BlockSpec(shape, lambda v: (0,) * len(shape))
+        return pl.pallas_call(
+            update,
+            grid=(V,),
+            out_shape=(
+                jax.ShapeDtypeStruct(amplitudes.shape, f32),
+                jax.ShapeDtypeStruct((2, modes), f32),
+            ),
+            in_specs=[
+                pl.BlockSpec((CY, 4 * NB), lambda v: (v, 0)),
+                pl.BlockSpec((CY, 16), lambda v: (v, 0)),
+                whole((WALL, 16, 128)),
+                whole((8, 128)),
+                whole((8, 128)),
+            ],
+            out_specs=(
+                pl.BlockSpec((2, 1, CY, 2 * NB), lambda v: (0, v, 0, 0)),
+                whole((2, modes)),
+            ),
+        )(acc, zmat, near, inner, weight)
 
     placed = (
         P(None, None, "wall", ("freq", "span")),

time: 115 us -> 105 us (0.913)
  local copies, waits for them, and re-layouts: 9.46 us -> 0 us
    unnamed x9 -> x0, local copies, waits for them, and re-layouts: 9.46 us -> none
    pallas_call x1 -> x2, Pallas kernels: 105 us -> 104 us  [the longest x1 99.2 us: local(): pl.pallas_call(kernel, out_shape=(jax.ShapeDtypeStruct((EXT, 4 * NB), f32...]
where the time goes in v2:
time: 105 us; the launch traced here: 104 us
  Pallas kernels  104 us (99%)
    pallas_call x1, Pallas kernels, local(): pl.pallas_call(kernel, out_shape=(jax.ShapeDtypeStruct((EXT, 4 * NB), f32...  99.2 us
    pallas_call x1, Pallas kernels, local(): pl.pallas_call(update, grid=(V,), out_shape=(jax.ShapeDtypeStruct(amplitu...  4.54 us

profile of v2, /device:TPU:1, one launch (start us, length us, event | category | flops | bytes accessed | tf_op | source)
XLA Modules:
  0.0 104.3 jit_solution(13786559589935052249)
XLA Ops:
  0.6 99.2 %shard_map.167 = (f32[320,1024]{1,0:T(8,128)}, f32[320,16]{1,0:T(8,128)}, f32[8,16,128]{2,1,0:T(8,128)}, f32[8,128]{1,0:T(8,128)}, f32[8,128]{1,0:T(8,128)}) custom-call(f32[2,5,64,512]{3,2,1,0:T(8,128)} %amp_hbm.1, f32[2,5,64,512]{3,2,1,0:T(8,128)} %up_hbm.1, s32[1,512]{1,0:T(1,128)} %bitcast.11, f32[5,5,5]{2,1,0:T(8,128)} %quad_ref.1, ...), custom_call_target="tpu_custom_call" | custom-call | tf_op jit(solution)/shard_map/pallas_call | solution.py:432
  99.8 4.5 %shard_map.168 = (f32[2,5,64,512]{3,2,1,0:T(8,128)}, f32[2,512]{1,0:T(2,128)}) custom-call(f32[320,1024]{1,0:T(8,128)} %get-tuple-element.7.acc_ref, f32[320,16]{1,0:T(8,128)} %get-tuple-element.8.zmat_ref, f32[8,16,128]{2,1,0:T(8,128)} %get-tuple-element.9.near_ref, f32[8,128]{1,0:T(8,128)} %get-tuple-element.10.inner_ref, ...), custom_call_target="tpu_custom_call" | custom-call | tf_op jit(solution)/shard_map/pallas_call | solution.py:495

commit v3 on v2

--- a/solution.py
+++ b/solution.py
@@ -73,11 +73,12 @@
 
 
 def kernel(
-    amp_hbm, up_hbm, mask_ref, quad_ref, inv_hbm, lower_ref, upper_ref, rlow_ref, rup_ref, rpiv_ref,
-    th_hbm, tl_hbm, ch_ref, cl_ref, dh_ref, dl_ref,
-    acc_hbm, zmat, nrecv, inner_ref, weight_ref,
-    amp_ref, up_ref, inv_ref, th_ref, tl_ref,
-    kh, kl, send1, recv1, send2, recv2, invs, ph, pl_, su, et, acc, mixed, eacc, pacc, mm,
+    amp_hbm, up_hbm, mask_hbm, quad_hbm, inv_hbm, lower_hbm, upper_hbm, rlow_hbm, rup_hbm, rpiv_hbm,
+    th_hbm, tl_hbm, ch_hbm, cl_hbm, dh_hbm, dl_hbm,
+    acc, zmat, nrecv, inner_ref, weight_ref,
+    amp_ref, up_ref, mask_ref, quad_ref, inv_ref, lower_ref, upper_ref, rlow_ref, rup_ref, rpiv_ref,
+    th_ref, tl_ref, ch_ref, cl_ref, dh_ref, dl_ref,
+    kh, kl, send1, recv1, send2, recv2, invs, ph, pl_, su, et, mixed, eacc, pacc, mm,
     wsend, wrecv, msend, mrecv, bsend, brecv, lsend, lrecv, nsend, invb_h, invb_l,
     s1, r1, s2, r2, sw, rw, loads,
 ):
@@ -89,9 +90,15 @@
     fetch = [
         pltpu.make_async_copy(amp_hbm.at[:, v], amp_ref.at[:, v], loads.at[v]) for v in range(V)
     ]
-    for src, dst in ((th_hbm, th_ref), (tl_hbm, tl_ref), (inv_hbm, inv_ref), (up_hbm, up_ref)):
+    for src, dst in (
+        (th_hbm, th_ref), (tl_hbm, tl_ref), (mask_hbm, mask_ref), (rlow_hbm, rlow_ref),
+        (rup_hbm, rup_ref), (rpiv_hbm, rpiv_ref), (lower_hbm, lower_ref), (upper_hbm, upper_ref),
+        (inv_hbm, inv_ref), (up_hbm, up_ref), (quad_hbm, quad_ref), (ch_hbm, ch_ref),
+        (cl_hbm, cl_ref), (dh_hbm, dh_ref), (dl_hbm, dl_ref),
+    ):
         fetch.append(pltpu.make_async_copy(src, dst, loads.at[len(fetch)]))
-    for copy in fetch:
+    fetch[V + 2].start()
+    for copy in fetch[: V + 2] + fetch[V + 3 :]:
         copy.start()
 
     def peer(i):
@@ -151,6 +158,7 @@
             recv_sem=rw.at[step, p if inbound else w], device_id={"wall": p}, device_id_type=MESH,
         )
 
+    fetch[V + 2].wait()
     keep = mask_ref[...].astype(jnp.float32)
 
     weight = jnp.zeros((1, 2 * NB), jnp.float32)
@@ -183,6 +191,8 @@
     exchange(send1, recv1, s1, r1)
     recv1[tile(me), :] = send1[tile(me), :]
 
+    for copy in fetch[V + 3 :]:
+        copy.wait()
     msend[...] = jnp.zeros_like(msend)
     msend[0:10, 0:10] = rlow_ref[:, 0]
     msend[16:26, 0:10] = rup_ref[:, 0]
@@ -193,7 +203,6 @@
         wall_copy(0, i, lambda p: msend, mrecv).start()
     mrecv[w] = msend[...]
 
-    fetch[V + 2].wait()
     invs[...] = jnp.zeros_like(invs)
     invs[:, 0:EXT] = inv_ref[0]
     row = lax.broadcasted_iota(jnp.int32, (16, 384), 0)
@@ -203,8 +212,8 @@
         for q in range(V):
             first = (row == q) & (col == v * CY)
             last = (row == V + q) & (col == v * CY + CY - 1)
-            ends = jnp.where(first, lower_ref[v, 0, q], ends)
-            ends = jnp.where(last, upper_ref[v, 0, q], ends)
+            ends = jnp.where(first, lower_ref[v, :, q : q + 1], ends)
+            ends = jnp.where(last, upper_ref[v, :, q : q + 1], ends)
     et[...] = ends
     zt = exact(et[...], invs[...], NT)
     zmat[...] = exact(invs[...], et[...], NT)
@@ -226,7 +235,6 @@
             high, low = split(jnp.where(inside, here if v % 2 == r else there, 0.0))
             ph[r * EXT : (r + 1) * EXT, 128 * v : 128 * (v + 1)] = high
             pl_[r * EXT : (r + 1) * EXT, 128 * v : 128 * (v + 1)] = low
-    fetch[V + 3].wait()
     inv_h, inv_l = split(inv_ref[0])
     for c in range(2):
         source = split(up_ref[c].reshape(EXT, 2 * NB))
@@ -285,17 +293,23 @@
             )
             found = product((ch_ref[parity], cl_ref[parity]), split(stacked), NN)
             mixed[z] = found if stage == 0 else mixed[z] + found
+    pairs = [(a, b) for a in range(V) for b in range(a + 1, V)]
+    weights = [[
+        jnp.broadcast_to(
+            quad_ref[o, a : a + 1, b : b + 1] + quad_ref[o, b : b + 1, a : a + 1], (8, 128)
+        ) for a, b in pairs
+    ] for o in range(V)]
     for z in range(4):
         field = []
         for v in range(V):
             x = mixed[z, :, 128 * v : 128 * (v + 1)]
-            field.append(pltpu.roll(x, CY, 1) + sign * x)
-        force = [jnp.zeros((GROUP, 128), jnp.float32) for _ in range(V)]
-        for a in range(V):
-            for b in range(a + 1, V):
-                both = field[a] * field[b]
-                for o in range(V):
-                    force[o] = force[o] + (quad_ref[o, a, b] + quad_ref[o, b, a]) * both
+            field.append((pltpu.roll(x, CY, 1) + sign * x).reshape(8, 8, 128))
+        force = [jnp.zeros((8, 8, 128), jnp.float32) for _ in range(V)]
+        for n, (a, b) in enumerate(pairs):
+            both = field[a] * field[b]
+            for o in range(V):
+                force[o] = force[o] + weights[o][n][None] * both
+        force = [x.reshape(GROUP, 128) for x in force]
         folded = jnp.concatenate([pltpu.roll(x, CY, 1) + sign * x for x in force], axis=1)
         stacked = jnp.concatenate(
             [jnp.where(halves, folded, 0.0), jnp.where(halves, 0.0, folded)], axis=0
@@ -352,8 +366,6 @@
             acc[:, at : at + NB] = (
                 pacc[r * EXT : (r + 1) * EXT, c * NB : (c + 1) * NB] + su[:, at : at + NB]
             ) * keep[:, r * NB : (r + 1) * NB]
-    store = pltpu.make_async_copy(acc, acc_hbm, loads.at[V + 4])
-    store.start()
     real = jnp.zeros((1, 2 * NB), jnp.float32)
     imag = jnp.zeros((1, 2 * NB), jnp.float32)
     for v in range(V):
@@ -392,25 +404,28 @@
         inner = inner + lrecv[i]
     inner_ref[...] = inner
     sent(send2, recv2, s2, r2)
-    store.wait()
     for i in range(1, WALL):
         wall_copy(4, i, lambda p: nsend.at[p], nrecv, True).wait()
 
 
-def update(acc_ref, zmat_ref, near_ref, inner_ref, weight_ref, new_ref, shift_ref):
+def update(acc_ref, zmat_ref, near_ref, inner_ref, weight_ref, new_hbm, shift_ref, new, sems):
     near = split(jnp.concatenate([near_ref[q] for q in range(WALL)], axis=1))
-    value = acc_ref[...] - product(split(zmat_ref[...]), near, NN)
-    new_ref[0, 0] = value[:, 0 : 2 * NB]
-    new_ref[1, 0] = value[:, 2 * NB : 4 * NB]
-
-    @pl.when(pl.program_id(0) == 0)
-    def _():
-        for q in range(4):
-            real = inner_ref[q : q + 1, :] - near_ref[q, 10:11, :] - near_ref[4 + q, 10:11, :]
-            imag = inner_ref[4 + q : 5 + q, :] - near_ref[q, 11:12, :] - near_ref[4 + q, 11:12, :]
-            size = weight_ref[q : q + 1, :]
-            shift_ref[0:1, 128 * q : 128 * (q + 1)] = imag / size
-            shift_ref[1:2, 128 * q : 128 * (q + 1)] = -real / size
+    stores = []
+    for v in range(V):
+        rows = slice(v * CY, (v + 1) * CY)
+        value = acc_ref[rows, :] - product(split(zmat_ref[rows, :]), near, NN)
+        new[0, v] = value[:, 0 : 2 * NB]
+        new[1, v] = value[:, 2 * NB : 4 * NB]
+        stores.append(pltpu.make_async_copy(new.at[:, v], new_hbm.at[:, v], sems.at[v]))
+        stores[-1].start()
+    for q in range(4):
+        real = inner_ref[q : q + 1, :] - near_ref[q, 10:11, :] - near_ref[4 + q, 10:11, :]
+        imag = inner_ref[4 + q : 5 + q, :] - near_ref[q, 11:12, :] - near_ref[4 + q, 11:12, :]
+        size = weight_ref[q : q + 1, :]
+        shift_ref[0:1, 128 * q : 128 * (q + 1)] = imag / size
+        shift_ref[1:2, 128 * q : 128 * (q + 1)] = -real / size
+    for store in stores:
+        store.wait()
 
 
 def solution(mesh):
@@ -421,10 +436,9 @@
         lower_coupling, upper_coupling, reduced_lower, reduced_upper, reduced_pivot,
     ):
         vmem = pl.BlockSpec(memory_space=pltpu.VMEM)
-        smem = pl.BlockSpec(memory_space=pltpu.SMEM)
         f32, bf16 = jnp.float32, jnp.bfloat16
         modes = amplitudes.shape[3]
-        hbm = pl.BlockSpec(memory_space=pl.ANY)
+        hbm = pl.BlockSpec(memory_space=pltpu.HBM)
 
         def turned(block):
             return jnp.transpose(block, (1, 0, 2))
@@ -438,15 +452,25 @@
                 jax.ShapeDtypeStruct((8, 128), f32),
                 jax.ShapeDtypeStruct((8, 128), f32),
             ),
-            in_specs=[hbm, hbm, vmem, smem, hbm, smem, smem, vmem, vmem, vmem]
-            + [hbm, hbm] + [vmem] * 4,
-            out_specs=(hbm, vmem, vmem, vmem, vmem),
+            in_specs=[hbm] * 16,
+            out_specs=(vmem,) * 5,
             scratch_shapes=[
                 pltpu.VMEM((2, V, CY, 2 * NB), f32),
                 pltpu.VMEM((2, V, CY, 2 * NB), f32),
+                pltpu.VMEM((1, modes), jnp.int32),
+                pltpu.VMEM((V, V, V), f32),
                 pltpu.VMEM((1, EXT, EXT), f32),
+                pltpu.VMEM((V, 1, V), f32),
+                pltpu.VMEM((V, 1, V), f32),
+                pltpu.VMEM((2 * V, 1, 2 * V), f32),
+                pltpu.VMEM((2 * V, 1, 2 * V), f32),
+                pltpu.VMEM((2 * V, 1, 2 * V), f32),
                 pltpu.VMEM((2 * NB, 2 * NB), bf16),
                 pltpu.VMEM((2 * NB, 2 * NB), bf16),
+                pltpu.VMEM((2, GROUP, 2 * GROUP), bf16),
+                pltpu.VMEM((2, GROUP, 2 * GROUP), bf16),
+                pltpu.VMEM((2 * GROUP, 2 * GROUP), bf16),
+                pltpu.VMEM((2 * GROUP, 2 * GROUP), bf16),
                 pltpu.VMEM((LANES, 2 * NB), bf16),
                 pltpu.VMEM((LANES, 2 * NB), bf16),
                 pltpu.VMEM((GROUP * MESSAGE, 128), f32),
@@ -458,7 +482,6 @@
                 pltpu.VMEM((2 * EXT, LANES), bf16),
                 pltpu.VMEM((EXT, 4 * NB), f32),
                 pltpu.VMEM((16, 384), f32),
-                pltpu.VMEM((EXT, 4 * NB), f32),
                 pltpu.VMEM((4, GROUP, LANES), f32),
                 pltpu.VMEM((32, 2 * NB), f32),
                 pltpu.VMEM((2 * EXT, 2 * NB), f32),
@@ -480,36 +503,30 @@
                 pltpu.SemaphoreType.DMA((GROUP,)),
                 pltpu.SemaphoreType.DMA((5, WALL)),
                 pltpu.SemaphoreType.DMA((5, WALL)),
-                pltpu.SemaphoreType.DMA((V + 5,)),
+                pltpu.SemaphoreType.DMA((V + 15,)),
             ],
             compiler_params=pltpu.CompilerParams(
-                collective_id=0, has_side_effects=True, vmem_limit_bytes=60 << 20
+                collective_id=0, has_side_effects=True, vmem_limit_bytes=40 << 20
             ),
-        )(
+        )(*[pltpu.with_memory_space_constraint(x, pltpu.HBM) for x in [
             amplitudes, upstream, harmonic_mask.reshape(1, modes), quadratic_coefficients,
             slab_inverse, turned(lower_coupling), turned(upper_coupling), turned(reduced_lower),
             turned(reduced_upper), turned(reduced_pivot),
             *[jnp.asarray(table) for table in consts],
-        )
-        whole = lambda shape: pl.BlockSpec(shape, lambda v: (0,) * len(shape))
+        ]])
         return pl.pallas_call(
             update,
-            grid=(V,),
             out_shape=(
                 jax.ShapeDtypeStruct(amplitudes.shape, f32),
                 jax.ShapeDtypeStruct((2, modes), f32),
             ),
-            in_specs=[
-                pl.BlockSpec((CY, 4 * NB), lambda v: (v, 0)),
-                pl.BlockSpec((CY, 16), lambda v: (v, 0)),
-                whole((WALL, 16, 128)),
-                whole((8, 128)),
-                whole((8, 128)),
+            in_specs=[vmem] * 5,
+            out_specs=(hbm, vmem),
+            scratch_shapes=[
+                pltpu.VMEM((2, V, CY, 2 * NB), f32),
+                pltpu.SemaphoreType.DMA((V,)),
             ],
-            out_specs=(
-                pl.BlockSpec((2, 1, CY, 2 * NB), lambda v: (0, v, 0, 0)),
-                whole((2, modes)),
-            ),
+            compiler_params=pltpu.CompilerParams(vmem_limit_bytes=16 << 20),
         )(acc, zmat, near, inner, weight)
 
     placed = (

time: 105 us -> 101 us (0.962)
  Pallas kernels: 104 us -> 99.8 us
    pallas_call x1, Pallas kernels: 4.54 us -> 1.98 us  [local(): pl.pallas_call(update, out_shape=(jax.ShapeDtypeStruct(amplitudes.shape,...]
    pallas_call x1, Pallas kernels: 99.2 us -> 97.8 us  [local(): pl.pallas_call(kernel, out_shape=(jax.ShapeDtypeStruct((EXT, 4 * NB), f32...]
where the time goes in v3:
time: 101 us; the launch traced here: 100 us
  Pallas kernels  99.8 us (99%)
    pallas_call x1, Pallas kernels, local(): pl.pallas_call(kernel, out_shape=(jax.ShapeDtypeStruct((EXT, 4 * NB), f32...  97.8 us

profile of v3, /device:TPU:1, one launch (start us, length us, event | category | flops | bytes accessed | tf_op | source)
XLA Modules:
  0.0 100.4 jit_solution(6036073009152069594)
XLA Ops:
  0.6 97.8 %shard_map.167 = (f32[320,1024]{1,0:T(8,128)S(1)}, f32[320,16]{1,0:T(8,128)S(1)}, f32[8,16,128]{2,1,0:T(8,128)S(1)}, f32[8,128]{1,0:T(8,128)S(1)}, f32[8,128]{1,0:T(8,128)S(1)}) custom-call(f32[2,5,64,512]{3,2,1,0:T(8,128)} %amp_hbm.1, f32[2,5,64,512]{3,2,1,0:T(8,128)} %up_hbm.1, s32[1,512]{1,0:T(1,128)} %bitcast.11, f32[5,5,5]{2,1,0:T(8,128)} %quad_hbm.1, ...), custom_call_target="tpu_custom_call" | custom-call | tf_op jit(solution)/shard_map/pallas_call | solution.py:446
  98.5 2.0 %shard_map.168 = (f32[2,5,64,512]{3,2,1,0:T(8,128)}, f32[2,512]{1,0:T(2,128)}) custom-call(f32[320,1024]{1,0:T(8,128)S(1)} %get-tuple-element.7.acc_ref, f32[320,16]{1,0:T(8,128)S(1)} %get-tuple-element.8.zmat_ref, f32[8,16,128]{2,1,0:T(8,128)S(1)} %get-tuple-element.9.near_ref, f32[8,128]{1,0:T(8,128)S(1)} %get-tuple-element.10.inner_ref, ...), custom_call_target="tpu_custom_call" | custom-call | tf_op jit(solution)/shard_map/pallas_call | solution.py:517

commit v4 on v3

--- a/solution.py
+++ b/solution.py
@@ -17,7 +17,8 @@
 GROUP = 64
 WALL = 8
 LANES = 2 * V * CY
-MESSAGE = 8 * V
+MESSAGE = 4 * V
+PITCH = 24
 EXT = V * CY
 epsilon = 1e-06
 HIGHEST = lax.Precision.HIGHEST
@@ -48,8 +49,8 @@
 def tables():
     scale = 1.0 / math.sqrt(NF * NB)
     n = np.arange(2 * NB)
-    z = 4 * (n // 8) + n % 4
-    d = (n // 4) % 2
+    z = 4 * (n // 4 % GROUP) + 2 * (n // (4 * GROUP)) + n % 2
+    d = (n // 2) % 2
     phase = 2.0 * np.pi * ((z[:, None] * np.arange(NB)[None, :]) % NB) / NB
     cos, sin = np.cos(phase), np.sin(phase)
     odd = (d == 1)[:, None]
@@ -60,11 +61,10 @@
     for r in range(2):
         phase = 2.0 * np.pi * ((t[:, None] * (2 * j + r)[None, :]) % NF) / NF
         pair = np.stack([np.cos(phase), -np.sin(phase)], axis=1) * scale
-        inverse.append(pair.reshape(GROUP, 2, 2, 32))
+        inverse.append(pair.reshape(GROUP, 2 * GROUP))
         forward.append(pair.reshape(GROUP, 2 * GROUP).T)
-    inverse = np.stack(inverse).transpose(3, 1, 0, 2, 4).reshape(2, GROUP, 2 * GROUP)
     out = []
-    for table in (span, inverse, np.concatenate(forward, axis=1)):
+    for table in (span, np.concatenate(inverse, axis=1), np.concatenate(forward, axis=1)):
         table = table.astype(np.float32)
         high = table.astype(jnp.bfloat16)
         low = (table - high.astype(np.float32)).astype(jnp.bfloat16)
@@ -78,7 +78,7 @@
     acc, zmat, nrecv, inner_ref, weight_ref,
     amp_ref, up_ref, mask_ref, quad_ref, inv_ref, lower_ref, upper_ref, rlow_ref, rup_ref, rpiv_ref,
     th_ref, tl_ref, ch_ref, cl_ref, dh_ref, dl_ref,
-    kh, kl, send1, recv1, send2, recv2, invs, ph, pl_, su, et, mixed, eacc, pacc, mm,
+    kh, kl, send1, recv1, send2, recv2, invs, ph, pl_, su, et, eacc, pacc, mm,
     wsend, wrecv, msend, mrecv, bsend, brecv, lsend, lrecv, nsend, invb_h, invb_l,
     s1, r1, s2, r2, sw, rw, loads,
 ):
@@ -117,39 +117,45 @@
     for i in range(1, WALL):
         pl.semaphore_signal(barrier, inc=1, device_id={"wall": (w + i) % WALL}, device_id_type=MESH)
 
-    def tile(index):
-        return pl.ds(pl.multiple_of(MESSAGE * index, 8), MESSAGE)
-
-    def message(i, src, dst, ssem, rsem, inbound):
+    def flat(half, index):
+        return pl.ds(pl.multiple_of(PITCH * (GROUP * half + index), 8), MESSAGE)
+
+    def paired(half, index):
+        return GROUP // 2 * half + index // 2, index % 2, pl.ds(0, MESSAGE)
+
+    def message(half, i, src, dst, src_at, dst_at, ssem, rsem, inbound):
         device, p = peer(i)
         at = p if inbound else me
         return pltpu.make_async_remote_copy(
-            src_ref=src.at[tile(p)], dst_ref=dst.at[tile(at)], send_sem=ssem.at[p],
-            recv_sem=rsem.at[at], device_id=device, device_id_type=MESH,
+            src_ref=src.at[src_at(half, p)], dst_ref=dst.at[dst_at(half, at)],
+            send_sem=ssem.at[half, p], recv_sem=rsem.at[half, at], device_id=device,
+            device_id_type=MESH,
         )
 
-    def exchange(*args):
+    out = (send1, recv1, paired, flat, s1, r1)
+    back = (send2, recv2, flat, paired, s2, r2)
+
+    def exchange(half, args):
         def go(i, carry):
-            message(i, *args, False).start()
+            message(half, i, *args, False).start()
             return carry
 
         lax.fori_loop(0, GROUP - 1, go, 0)
 
-    def arrive(first, last, *args):
+    def arrive(half, args):
         def done(i, carry):
-            message(i, *args, True).wait_recv()
+            message(half, i, *args, True).wait_recv()
             return carry
 
-        lax.fori_loop(first, last, done, 0)
-
-    def sent(*args):
+        lax.fori_loop(0, GROUP - 1, done, 0)
+
+    def sent(args):
         def done(i, carry):
-            message(i, *args, True).wait_send()
+            for half in range(2):
+                message(half, i, *args, True).wait_send()
             return carry
 
         lax.fori_loop(0, GROUP - 1, done, 0)
-
-    parts = ((core, 0, 31), (1 - core, 31, GROUP - 1))
 
     def wall_copy(step, i, src, dst, inbound=False):
         p = (w + i) % WALL
@@ -177,19 +183,36 @@
     fetch[V].wait()
     fetch[V + 1].wait()
 
+    upper_rows = lax.broadcasted_iota(jnp.int32, (16, 8, 128), 1) >= 4
+
+    def turn_rows(x):
+        return pltpu.roll(x, 4, 1)
+
+    def join(first, second, parity):
+        if parity == 0:
+            return jnp.where(upper_rows, turn_rows(second), first)
+        return jnp.where(upper_rows, second, turn_rows(first))
+
     def spectral(q, carry):
         rows = pl.ds(pl.multiple_of(128 * q, 128), 128)
         found = product((th_ref[rows, :], tl_ref[rows, :]), (kh[...], kl[...]), NT)
-        for p in range(16):
-            for v in range(V):
-                at = pl.multiple_of(16 * MESSAGE * q + MESSAGE * p + 8 * v, 8)
-                send1[pl.ds(at, 8), :] = found[8 * p : 8 * p + 8, 128 * v : 128 * v + 128]
+        tiles = [found[:, 128 * v : 128 * (v + 1)].reshape(16, 8, 128) for v in range(V)]
+        at = pl.ds(pl.multiple_of(16 * q, 16), 16)
+        for parity in range(2):
+            for n in range(2):
+                send1[at, parity, 8 * n : 8 * n + 8] = join(
+                    tiles[2 * n], tiles[2 * n + 1], parity
+                )
+            send1[at, parity, 16:24] = turn_rows(tiles[4]) if parity else tiles[4]
         return carry
 
-    lax.fori_loop(0, 4, spectral, 0)
+    lax.fori_loop(0, 2, spectral, 0)
     pl.semaphore_wait(barrier, GROUP - 1 + WALL - 1)
-    exchange(send1, recv1, s1, r1)
-    recv1[tile(me), :] = send1[tile(me), :]
+    exchange(0, out)
+    lax.fori_loop(2, 4, spectral, 0)
+    exchange(1, out)
+    for half in range(2):
+        recv1[flat(half, me), :] = send1[paired(half, me)]
 
     for copy in fetch[V + 3 :]:
         copy.wait()
@@ -278,31 +301,28 @@
 
     half = lax.broadcasted_iota(jnp.int32, (GROUP, 128), 1) < CY
     sign = jnp.where(half, 1.0, -1.0)
+    wide = lax.broadcasted_iota(jnp.int32, (128, LANES), 1) % 128 < CY
     halves = lax.broadcasted_iota(jnp.int32, (GROUP, LANES), 1) % 128 < CY
-    for stage, (parity, first, last) in enumerate(parts):
-        arrive(first, last, send1, recv1, s1, r1)
-        for z in range(4):
-            picked = jnp.concatenate([
-                jnp.concatenate([
-                    recv1[pl.ds(32 * MESSAGE * parity + 8 * v + 4 * d + z, 32, stride=MESSAGE), :]
-                    for v in range(V)
-                ], axis=1) for d in range(2)
-            ], axis=0)
-            stacked = jnp.concatenate(
-                [jnp.where(halves, picked, 0.0), jnp.where(halves, 0.0, picked)], axis=0
-            )
-            found = product((ch_ref[parity], cl_ref[parity]), split(stacked), NN)
-            mixed[z] = found if stage == 0 else mixed[z] + found
     pairs = [(a, b) for a in range(V) for b in range(a + 1, V)]
     weights = [[
         jnp.broadcast_to(
             quad_ref[o, a : a + 1, b : b + 1] + quad_ref[o, b : b + 1, a : a + 1], (8, 128)
         ) for a, b in pairs
     ] for o in range(V)]
-    for z in range(4):
+    def point(half, z):
+        start = PITCH * GROUP * half + z
+        picked = jnp.concatenate([
+            jnp.concatenate([
+                recv1[pl.ds(start + 4 * v + 2 * d, GROUP, stride=PITCH), :] for v in range(V)
+            ], axis=1) for d in range(2)
+        ], axis=0)
+        stacked = jnp.concatenate(
+            [jnp.where(wide, picked, 0.0), jnp.where(wide, 0.0, picked)], axis=0
+        )
+        mixed = product((ch_ref[...], cl_ref[...]), split(stacked), NN)
         field = []
         for v in range(V):
-            x = mixed[z, :, 128 * v : 128 * (v + 1)]
+            x = mixed[:, 128 * v : 128 * (v + 1)]
             field.append((pltpu.roll(x, CY, 1) + sign * x).reshape(8, 8, 128))
         force = [jnp.zeros((8, 8, 128), jnp.float32) for _ in range(V)]
         for n, (a, b) in enumerate(pairs):
@@ -314,28 +334,38 @@
         stacked = jnp.concatenate(
             [jnp.where(halves, folded, 0.0), jnp.where(halves, 0.0, folded)], axis=0
         )
-        back = product((dh_ref[...], dl_ref[...]), split(stacked), NN)
+        found = product((dh_ref[...], dl_ref[...]), split(stacked), NN)
         for v in range(V):
             for d in range(2):
-                send2[pl.ds(8 * v + 4 * d + z, GROUP, stride=MESSAGE), :] = back[
+                send2[pl.ds(start + 4 * v + 2 * d, GROUP, stride=PITCH), :] = found[
                     GROUP * d : GROUP * (d + 1), 128 * v : 128 * (v + 1)
                 ]
-    exchange(send2, recv2, s2, r2)
-    recv2[tile(me), :] = send2[tile(me), :]
-
-    sent(send1, recv1, s1, r1)
-    for stage, (parity, first, last) in enumerate(parts):
-        arrive(first, last, send2, recv2, s2, r2)
-        rows = pl.ds(pl.multiple_of(32 * MESSAGE * parity, 8), 32 * MESSAGE)
-        landed = recv2[rows, :].reshape(32, V, 8, 128)
-        arrived = split(
-            jnp.concatenate([landed[:, v].reshape(2 * 128, 128) for v in range(V)], axis=1)
-        )
-        rows = pl.ds(pl.multiple_of(256 * parity, 256), 256)
+
+    for half in range(2):
+        arrive(half, out)
+        for z in range(2):
+            point(half, z)
+        exchange(half, back)
+        recv2[paired(half, me)] = send2[flat(half, me), :]
+
+    sent(out)
+    upper_rows = lax.broadcasted_iota(jnp.int32, (32, 8, 128), 1) >= 4
+    for half in range(2):
+        arrive(half, back)
+        even, odd = recv2[32 * half : 32 * half + 32, 0], recv2[32 * half : 32 * half + 32, 1]
+        tiles = []
+        for v in range(V):
+            near, far = (x[:, 8 * (v // 2) : 8 * (v // 2) + 8] for x in (even, odd))
+            if v % 2 == 0:
+                tiles.append(jnp.where(upper_rows, turn_rows(far), near))
+            else:
+                tiles.append(jnp.where(upper_rows, far, turn_rows(near)))
+        arrived = split(jnp.concatenate([x.reshape(256, 128) for x in tiles], axis=1))
+        rows = pl.ds(256 * half, 256)
         table = (th_ref[rows, :], tl_ref[rows, :])
         found = product((invb_h[...], invb_l[...]), arrived, NT)
         found = product(split(found), table, NN)
-        if stage == 0:
+        if half == 0:
             eacc[...] = found
             found = product((ph[...], pl_[...]), arrived, NT)
             pacc[...] = product(split(found), table, NN)
@@ -403,7 +433,7 @@
     for i in range(1, WALL):
         inner = inner + lrecv[i]
     inner_ref[...] = inner
-    sent(send2, recv2, s2, r2)
+    sent(back)
     for i in range(1, WALL):
         wall_copy(4, i, lambda p: nsend.at[p], nrecv, True).wait()
 
@@ -467,22 +497,21 @@
                 pltpu.VMEM((2 * V, 1, 2 * V), f32),
                 pltpu.VMEM((2 * NB, 2 * NB), bf16),
                 pltpu.VMEM((2 * NB, 2 * NB), bf16),
-                pltpu.VMEM((2, GROUP, 2 * GROUP), bf16),
-                pltpu.VMEM((2, GROUP, 2 * GROUP), bf16),
+                pltpu.VMEM((GROUP, 4 * GROUP), bf16),
+                pltpu.VMEM((GROUP, 4 * GROUP), bf16),
                 pltpu.VMEM((2 * GROUP, 2 * GROUP), bf16),
                 pltpu.VMEM((2 * GROUP, 2 * GROUP), bf16),
                 pltpu.VMEM((LANES, 2 * NB), bf16),
                 pltpu.VMEM((LANES, 2 * NB), bf16),
-                pltpu.VMEM((GROUP * MESSAGE, 128), f32),
-                pltpu.VMEM((GROUP * MESSAGE, 128), f32),
-                pltpu.VMEM((GROUP * MESSAGE, 128), f32),
-                pltpu.VMEM((GROUP * MESSAGE, 128), f32),
+                pltpu.VMEM((GROUP, 2, PITCH, 128), f32),
+                pltpu.VMEM((2 * GROUP * PITCH, 128), f32),
+                pltpu.VMEM((2 * GROUP * PITCH, 128), f32),
+                pltpu.VMEM((GROUP, 2, PITCH, 128), f32),
                 pltpu.VMEM((EXT, 384), f32),
                 pltpu.VMEM((2 * EXT, LANES), bf16),
                 pltpu.VMEM((2 * EXT, LANES), bf16),
                 pltpu.VMEM((EXT, 4 * NB), f32),
                 pltpu.VMEM((16, 384), f32),
-                pltpu.VMEM((4, GROUP, LANES), f32),
                 pltpu.VMEM((32, 2 * NB), f32),
                 pltpu.VMEM((2 * EXT, 2 * NB), f32),
                 pltpu.VMEM((128, 128), f32),
@@ -497,10 +526,10 @@
                 pltpu.VMEM((WALL, 16, 128), f32),
                 pltpu.VMEM((32, LANES), bf16),
                 pltpu.VMEM((32, LANES), bf16),
-                pltpu.SemaphoreType.DMA((GROUP,)),
-                pltpu.SemaphoreType.DMA((GROUP,)),
-                pltpu.SemaphoreType.DMA((GROUP,)),
-                pltpu.SemaphoreType.DMA((GROUP,)),
+                pltpu.SemaphoreType.DMA((2, GROUP)),
+                pltpu.SemaphoreType.DMA((2, GROUP)),
+                pltpu.SemaphoreType.DMA((2, GROUP)),
+                pltpu.SemaphoreType.DMA((2, GROUP)),
                 pltpu.SemaphoreType.DMA((5, WALL)),
                 pltpu.SemaphoreType.DMA((5, WALL)),
                 pltpu.SemaphoreType.DMA((V + 15,)),

time: 101 us -> 96.8 us (0.958)
  Pallas kernels: 99.8 us -> 96.1 us
    pallas_call x1, Pallas kernels: 97.8 us -> 94.1 us  [local(): pl.pallas_call(kernel, out_shape=(jax.ShapeDtypeStruct((EXT, 4 * NB), f32...]
where the time goes in v4:
time: 96.8 us; the launch traced here: 96.7 us
  Pallas kernels  96.1 us (99%)
    pallas_call x1, Pallas kernels, local(): pl.pallas_call(kernel, out_shape=(jax.ShapeDtypeStruct((EXT, 4 * NB), f32...  94.1 us
    pallas_call x1, Pallas kernels, local(): pl.pallas_call(update, out_shape=(jax.ShapeDtypeStruct(amplitudes.shape,...  1.99 us

profile of v4, /device:TPU:1, one launch (start us, length us, event | category | flops | bytes accessed | tf_op | source)
XLA Modules:
  0.0 96.7 jit_solution(11705157093309135888)
XLA Ops:
  0.6 94.1 %shard_map.167 = (f32[320,1024]{1,0:T(8,128)S(1)}, f32[320,16]{1,0:T(8,128)S(1)}, f32[8,16,128]{2,1,0:T(8,128)S(1)}, f32[8,128]{1,0:T(8,128)S(1)}, f32[8,128]{1,0:T(8,128)S(1)}) custom-call(f32[2,5,64,512]{3,2,1,0:T(8,128)} %amp_hbm.1, f32[2,5,64,512]{3,2,1,0:T(8,128)} %up_hbm.1, s32[1,512]{1,0:T(1,128)} %bitcast.11, f32[5,5,5]{2,1,0:T(8,128)} %quad_hbm.1, ...), custom_call_target="tpu_custom_call" | custom-call | tf_op jit(solution)/shard_map/pallas_call | solution.py:476
  94.7 2.0 %shard_map.168 = (f32[2,5,64,512]{3,2,1,0:T(8,128)}, f32[2,512]{1,0:T(2,128)}) custom-call(f32[320,1024]{1,0:T(8,128)S(1)} %get-tuple-element.7.acc_ref, f32[320,16]{1,0:T(8,128)S(1)} %get-tuple-element.8.zmat_ref, f32[8,16,128]{2,1,0:T(8,128)S(1)} %get-tuple-element.9.near_ref, f32[8,128]{1,0:T(8,128)S(1)} %get-tuple-element.10.inner_ref, ...), custom_call_target="tpu_custom_call" | custom-call | tf_op jit(solution)/shard_map/pallas_call | solution.py:546

commit v5 on v4

--- a/solution.py
+++ b/solution.py
@@ -78,7 +78,7 @@
     acc, zmat, nrecv, inner_ref, weight_ref,
     amp_ref, up_ref, mask_ref, quad_ref, inv_ref, lower_ref, upper_ref, rlow_ref, rup_ref, rpiv_ref,
     th_ref, tl_ref, ch_ref, cl_ref, dh_ref, dl_ref,
-    kh, kl, send1, recv1, send2, recv2, invs, ph, pl_, su, et, eacc, pacc, mm,
+    kh, kl, send1, recv1, send2, recv2, invs, ph, pl_, su, et, eacc, esource, ekeep, pacc, mm,
     wsend, wrecv, msend, mrecv, bsend, brecv, lsend, lrecv, nsend, invb_h, invb_l,
     s1, r1, s2, r2, sw, rw, loads,
 ):
@@ -101,19 +101,22 @@
     for copy in fetch[: V + 2] + fetch[V + 3 :]:
         copy.start()
 
-    def peer(i):
-        i = jnp.where(i >= 7, i + 1, i)
-        n = 7 - i % 8
-        dz = (n % 2) * ((n + 1) // 2) + (1 - n % 2) * ((8 - n // 2) % 8)
-        df, dc = (i // 8) % 4, i // 32
-        pf, pc, pz = (f + df) % 4, (core + dc) % 2, (chip + dz) % 8
-        return {"freq": pf, "span": pz * 2 + pc}, pc * 32 + pf * 8 + pz
-
-    def greet(i, carry):
-        pl.semaphore_signal(barrier, inc=1, device_id=peer(i)[0], device_id_type=MESH)
-        return carry
-
-    lax.fori_loop(0, GROUP - 1, greet, 0)
+    spot = f * 8 + chip
+
+    def everyone(act):
+        for other in range(2):
+            c = core if other == 0 else 1 - core
+
+            def one(i, carry):
+                p = lax.rem(spot + i, 32)
+                act({"freq": lax.div(p, 8), "span": 2 * lax.rem(p, 8) + c}, 32 * c + p)
+                return carry
+
+            lax.fori_loop(1 - other, 32, one, 0)
+
+    everyone(
+        lambda device, p: pl.semaphore_signal(barrier, inc=1, device_id=device, device_id_type=MESH)
+    )
     for i in range(1, WALL):
         pl.semaphore_signal(barrier, inc=1, device_id={"wall": (w + i) % WALL}, device_id_type=MESH)
 
@@ -121,11 +124,9 @@
         return pl.ds(pl.multiple_of(PITCH * (GROUP * half + index), 8), MESSAGE)
 
     def paired(half, index):
-        return GROUP // 2 * half + index // 2, index % 2, pl.ds(0, MESSAGE)
-
-    def message(half, i, src, dst, src_at, dst_at, ssem, rsem, inbound):
-        device, p = peer(i)
-        at = p if inbound else me
+        return GROUP // 2 * half + lax.div(index, 2), lax.rem(index, 2), pl.ds(0, MESSAGE)
+
+    def message(half, device, p, at, src, dst, src_at, dst_at, ssem, rsem):
         return pltpu.make_async_remote_copy(
             src_ref=src.at[src_at(half, p)], dst_ref=dst.at[dst_at(half, at)],
             send_sem=ssem.at[half, p], recv_sem=rsem.at[half, at], device_id=device,
@@ -136,26 +137,14 @@
     back = (send2, recv2, flat, paired, s2, r2)
 
     def exchange(half, args):
-        def go(i, carry):
-            message(half, i, *args, False).start()
-            return carry
-
-        lax.fori_loop(0, GROUP - 1, go, 0)
+        everyone(lambda device, p: message(half, device, p, me, *args).start())
 
     def arrive(half, args):
-        def done(i, carry):
-            message(half, i, *args, True).wait_recv()
-            return carry
-
-        lax.fori_loop(0, GROUP - 1, done, 0)
+        everyone(lambda device, p: message(half, device, p, p, *args).wait_recv())
 
     def sent(args):
-        def done(i, carry):
-            for half in range(2):
-                message(half, i, *args, True).wait_send()
-            return carry
-
-        lax.fori_loop(0, GROUP - 1, done, 0)
+        for half in range(2):
+            everyone(lambda device, p: message(half, device, p, p, *args).wait_send())
 
     def wall_copy(step, i, src, dst, inbound=False):
         p = (w + i) % WALL
@@ -296,6 +285,16 @@
                 to, at = 16 * r + e * V + v, r * EXT + v * CY + e * (CY - 1)
                 invb_h[to : to + 1, :] = ph[at : at + 1, :]
                 invb_l[to : to + 1, :] = pl_[at : at + 1, :]
+    esource[...] = jnp.zeros_like(esource)
+    for r in range(2):
+        used = keep[:, r * NB : (r + 1) * NB]
+        for c in range(2):
+            ekeep[16 * r : 16 * (r + 1), c * NB : (c + 1) * NB] = jnp.broadcast_to(used, (16, NB))
+            at = c * 2 * NB + r * NB
+            for e in range(2):
+                for v in range(V):
+                    to, o = 16 * r + e * V + v, v * CY + e * (CY - 1)
+                    esource[to : to + 1, c * NB : (c + 1) * NB] = su[o : o + 1, at : at + NB] * used
     for i in range(1, WALL):
         wall_copy(1, i, lambda p: wsend.at[p % 4], wrecv, True).wait()
 
@@ -369,22 +368,12 @@
             eacc[...] = found
             found = product((ph[...], pl_[...]), arrived, NT)
             pacc[...] = product(split(found), table, NN)
-    edges = eacc[...] + found
+    edges = (eacc[...] + found) * ekeep[...] + esource[...]
     for r in range(2):
-        edge = edges[16 * r : 16 * (r + 1)]
         for c in range(2):
             for q in range(2):
-                at = r * NB + q * 128
-                part = edge[:, c * NB + q * 128 : c * NB + (q + 1) * 128]
-                for e in range(2):
-                    for v in range(V):
-                        o = v * CY + e * (CY - 1)
-                        bsend[c * 4 + r * 2 + q, e * V + v : e * V + v + 1, :] = (
-                            part[e * V + v : e * V + v + 1, :]
-                            + su[o : o + 1, c * 2 * NB + at : c * 2 * NB + at + 128]
-                        ) * keep[:, at : at + 128]
-    for q in range(WALL):
-        bsend[q, 2 * V : 16, :] = jnp.zeros((16 - 2 * V, 128), jnp.float32)
+                at = c * NB + q * 128
+                bsend[c * 4 + r * 2 + q] = edges[16 * r : 16 * (r + 1), at : at + 128]
     for i in range(1, WALL):
         wall_copy(2, i, lambda p: bsend.at[p], brecv).start()
     brecv[w] = bsend[w]
@@ -512,6 +501,8 @@
                 pltpu.VMEM((2 * EXT, LANES), bf16),
                 pltpu.VMEM((EXT, 4 * NB), f32),
                 pltpu.VMEM((16, 384), f32),
+                pltpu.VMEM((32, 2 * NB), f32),
+                pltpu.VMEM((32, 2 * NB), f32),
                 pltpu.VMEM((32, 2 * NB), f32),
                 pltpu.VMEM((2 * EXT, 2 * NB), f32),
                 pltpu.VMEM((128, 128), f32),

time: 96.8 us -> 94 us (0.971)
  Pallas kernels: 96.1 us -> 93.3 us
    pallas_call x1, Pallas kernels: 94.1 us -> 91.3 us  [local(): pl.pallas_call(kernel, out_shape=(jax.ShapeDtypeStruct((EXT, 4 * NB), f32...]
where the time goes in v5:
time: 94 us; the launch traced here: 93.9 us
  Pallas kernels  93.3 us (99%)
    pallas_call x1, Pallas kernels, local(): pl.pallas_call(kernel, out_shape=(jax.ShapeDtypeStruct((EXT, 4 * NB), f32...  91.3 us
    pallas_call x1, Pallas kernels, local(): pl.pallas_call(update, out_shape=(jax.ShapeDtypeStruct(amplitudes.shape,...  1.98 us

profile of v5, /device:TPU:1, one launch (start us, length us, event | category | flops | bytes accessed | tf_op | source)
XLA Modules:
  0.0 93.9 jit_solution(4856073624776129207)
XLA Ops:
  0.6 91.3 %shard_map.167 = (f32[320,1024]{1,0:T(8,128)S(1)}, f32[320,16]{1,0:T(8,128)S(1)}, f32[8,16,128]{2,1,0:T(8,128)S(1)}, f32[8,128]{1,0:T(8,128)S(1)}, f32[8,128]{1,0:T(8,128)S(1)}) custom-call(f32[2,5,64,512]{3,2,1,0:T(8,128)} %amp_hbm.1, f32[2,5,64,512]{3,2,1,0:T(8,128)} %up_hbm.1, s32[1,512]{1,0:T(1,128)} %bitcast.11, f32[5,5,5]{2,1,0:T(8,128)} %quad_hbm.1, ...), custom_call_target="tpu_custom_call" | custom-call | tf_op jit(solution)/shard_map/pallas_call | solution.py:465
  91.9 2.0 %shard_map.168 = (f32[2,5,64,512]{3,2,1,0:T(8,128)}, f32[2,512]{1,0:T(2,128)}) custom-call(f32[320,1024]{1,0:T(8,128)S(1)} %get-tuple-element.7.acc_ref, f32[320,16]{1,0:T(8,128)S(1)} %get-tuple-element.8.zmat_ref, f32[8,16,128]{2,1,0:T(8,128)S(1)} %get-tuple-element.9.near_ref, f32[8,128]{1,0:T(8,128)S(1)} %get-tuple-element.10.inner_ref, ...), custom_call_target="tpu_custom_call" | custom-call | tf_op jit(solution)/shard_map/pallas_call | solution.py:537

commit v6 on v5

--- a/solution.py
+++ b/solution.py
@@ -103,8 +103,8 @@
 
     spot = f * 8 + chip
 
-    def everyone(act):
-        for other in range(2):
+    def everyone(act, groups=(0, 1)):
+        for other in groups:
             c = core if other == 0 else 1 - core
 
             def one(i, carry):
@@ -136,11 +136,11 @@
     out = (send1, recv1, paired, flat, s1, r1)
     back = (send2, recv2, flat, paired, s2, r2)
 
-    def exchange(half, args):
-        everyone(lambda device, p: message(half, device, p, me, *args).start())
-
-    def arrive(half, args):
-        everyone(lambda device, p: message(half, device, p, p, *args).wait_recv())
+    def exchange(half, args, groups=(0, 1)):
+        everyone(lambda device, p: message(half, device, p, me, *args).start(), groups)
+
+    def arrive(half, args, groups=(0, 1)):
+        everyone(lambda device, p: message(half, device, p, p, *args).wait_recv(), groups)
 
     def sent(args):
         for half in range(2):
@@ -182,7 +182,7 @@
             return jnp.where(upper_rows, turn_rows(second), first)
         return jnp.where(upper_rows, second, turn_rows(first))
 
-    def spectral(q, carry):
+    def spectral(q):
         rows = pl.ds(pl.multiple_of(128 * q, 128), 128)
         found = product((th_ref[rows, :], tl_ref[rows, :]), (kh[...], kl[...]), NT)
         tiles = [found[:, 128 * v : 128 * (v + 1)].reshape(16, 8, 128) for v in range(V)]
@@ -193,13 +193,13 @@
                     tiles[2 * n], tiles[2 * n + 1], parity
                 )
             send1[at, parity, 16:24] = turn_rows(tiles[4]) if parity else tiles[4]
-        return carry
-
-    lax.fori_loop(0, 2, spectral, 0)
-    pl.semaphore_wait(barrier, GROUP - 1 + WALL - 1)
-    exchange(0, out)
-    lax.fori_loop(2, 4, spectral, 0)
-    exchange(1, out)
+
+    for half in range(2):
+        for group, parity in enumerate((core, 1 - core)):
+            spectral(2 * half + parity)
+            if half == 0 and group == 0:
+                pl.semaphore_wait(barrier, GROUP - 1 + WALL - 1)
+            exchange(half, out, (group,))
     for half in range(2):
         recv1[flat(half, me), :] = send1[paired(half, me)]
 
@@ -348,10 +348,12 @@
         recv2[paired(half, me)] = send2[flat(half, me), :]
 
     sent(out)
-    upper_rows = lax.broadcasted_iota(jnp.int32, (32, 8, 128), 1) >= 4
-    for half in range(2):
-        arrive(half, back)
-        even, odd = recv2[32 * half : 32 * half + 32, 0], recv2[32 * half : 32 * half + 32, 1]
+    for stage in range(4):
+        half, group = stage // 2, stage % 2
+        parity = core if group == 0 else 1 - core
+        arrive(half, back, (group,))
+        rows = pl.ds(pl.multiple_of(32 * half + 16 * parity, 16), 16)
+        even, odd = recv2[rows, 0], recv2[rows, 1]
         tiles = []
         for v in range(V):
             near, far = (x[:, 8 * (v // 2) : 8 * (v // 2) + 8] for x in (even, odd))
@@ -359,15 +361,16 @@
                 tiles.append(jnp.where(upper_rows, turn_rows(far), near))
             else:
                 tiles.append(jnp.where(upper_rows, far, turn_rows(near)))
-        arrived = split(jnp.concatenate([x.reshape(256, 128) for x in tiles], axis=1))
-        rows = pl.ds(256 * half, 256)
+        arrived = split(jnp.concatenate([x.reshape(128, 128) for x in tiles], axis=1))
+        rows = pl.ds(pl.multiple_of(256 * half + 128 * parity, 128), 128)
         table = (th_ref[rows, :], tl_ref[rows, :])
         found = product((invb_h[...], invb_l[...]), arrived, NT)
         found = product(split(found), table, NN)
-        if half == 0:
-            eacc[...] = found
+        if stage < 3:
+            eacc[...] = found if stage == 0 else eacc[...] + found
             found = product((ph[...], pl_[...]), arrived, NT)
-            pacc[...] = product(split(found), table, NN)
+            found = product(split(found), table, NN)
+            pacc[...] = found if stage == 0 else pacc[...] + found
     edges = (eacc[...] + found) * ekeep[...] + esource[...]
     for r in range(2):
         for c in range(2):
@@ -493,8 +496,8 @@
                 pltpu.VMEM((LANES, 2 * NB), bf16),
                 pltpu.VMEM((LANES, 2 * NB), bf16),
                 pltpu.VMEM((GROUP, 2, PITCH, 128), f32),
-                pltpu.VMEM((2 * GROUP * PITCH, 128), f32),
-                pltpu.VMEM((2 * GROUP * PITCH, 128), f32),
+                pltpu.VMEM(((2 * GROUP + 1) * PITCH, 128), f32),
+                pltpu.VMEM(((2 * GROUP + 1) * PITCH, 128), f32),
                 pltpu.VMEM((GROUP, 2, PITCH, 128), f32),
                 pltpu.VMEM((EXT, 384), f32),
                 pltpu.VMEM((2 * EXT, LANES), bf16),

time: 94 us -> 93.8 us (level)
  no operation moved by 1% of the time
where the time goes in v6:
time: 93.8 us; the launch traced here: 93.7 us
  Pallas kernels  92.9 us (99%)
    pallas_call x1, Pallas kernels, local(): pl.pallas_call(kernel, out_shape=(jax.ShapeDtypeStruct((EXT, 4 * NB), f32...  90.9 us
    pallas_call x1, Pallas kernels, local(): pl.pallas_call(update, out_shape=(jax.ShapeDtypeStruct(amplitudes.shape,...  1.98 us

profile of v6, /device:TPU:1, one launch (start us, length us, event | category | flops | bytes accessed | tf_op | source)
XLA Modules:
  0.0 93.7 jit_solution(11020622051074543663)
XLA Ops:
  0.6 90.9 %shard_map.167 = (f32[320,1024]{1,0:T(8,128)S(1)}, f32[320,16]{1,0:T(8,128)S(1)}, f32[8,16,128]{2,1,0:T(8,128)S(1)}, f32[8,128]{1,0:T(8,128)S(1)}, f32[8,128]{1,0:T(8,128)S(1)}) custom-call(f32[2,5,64,512]{3,2,1,0:T(8,128)} %amp_hbm.1, f32[2,5,64,512]{3,2,1,0:T(8,128)} %up_hbm.1, s32[1,512]{1,0:T(1,128)} %bitcast.11, f32[5,5,5]{2,1,0:T(8,128)} %quad_hbm.1, ...), custom_call_target="tpu_custom_call" | custom-call | tf_op jit(solution)/shard_map/pallas_call | solution.py:468
  91.5 2.0 %shard_map.168 = (f32[2,5,64,512]{3,2,1,0:T(8,128)}, f32[2,512]{1,0:T(2,128)}) custom-call(f32[320,1024]{1,0:T(8,128)S(1)} %get-tuple-element.7.acc_ref, f32[320,16]{1,0:T(8,128)S(1)} %get-tuple-element.8.zmat_ref, f32[8,16,128]{2,1,0:T(8,128)S(1)} %get-tuple-element.9.near_ref, f32[8,128]{1,0:T(8,128)S(1)} %get-tuple-element.10.inner_ref, ...), custom_call_target="tpu_custom_call" | custom-call | tf_op jit(solution)/shard_map/pallas_call | solution.py:540
